TPU v7x, 32 devices: a whole 2x2x4 slice. The times are simulated.
32 devices in a mesh: gx: 4 (over x, core), gy: 8 (over z, y).
Axes of the slice: x: 2, y: 2, z: 4, core: 2. Of those that a mesh axis runs over, the one named last changes fastest.
Arguments:
- increment: float32 [8, 2048, 1024], P(None, 'gx', 'gy'), may hold values from -6 to 6
- deviation: float32 [8, 2048, 1024], P(None, 'gx', 'gy'), may hold values from 0.5 to 2
- land_sea: int32 [8, 2048, 1024], P(None, 'gx', 'gy'), may hold values 0 or 1
- filter_steps: int32 [8], replicated, may hold values from 1 to 2, as said below
- zonal_rate: float32 [8], replicated, may hold values from 0.0009765625 to 0.03
- meridional_rate: float32 [8], replicated, may hold values from 0.001953125 to 0.03
Outputs:
- covaried: float32 [8, 2048, 1024], P(None, 'gx', 'gy')
Inputs may be any that keep to these rules, and one draw needn't show every extreme that they name: `filter_steps`: some level has 2 repetitions and some level has 1.
All inputs are finite; a program needn't handle non-finite values. No bound on the sum of `land_sea` on one device may be relied on, other than what follows from the above.
Results may differ from a plain program's by a relative error of at most 0.0003.
Values sent between devices are 32-bit elements; how exact they have to be, the bound alone decides.
A program may use at most 128 MiB of HBM per device.

v0:
```python
import functools

import jax
import jax.numpy as jnp
from jax import lax
from jax.experimental import pallas as pl
from jax.experimental.pallas import tpu as pltpu
from jax.sharding import PartitionSpec as P

BX = 256
MAXSTEPS = 2
UNROLL = 2
gain_base = 3.0**0.125
MESH = pl.DeviceIdType.MESH
f32, bf16 = jnp.float32, jnp.bfloat16


def section_gain(decay_rate, filter_steps):
    fading = -jnp.expm1(-decay_rate)
    return gain_base * fading ** (1.0 - 1.0 / (16.0 * filter_steps.astype(f32)))


def binomials(count):
    return (
        jnp.ones_like(count),
        count,
        count * (count + 1.0) / 2.0,
        count * (count + 1.0) * (count + 2.0) / 6.0,
    )


def by_row(values, row):
    total = jnp.zeros(row.shape, f32)
    for k, value in enumerate(values):
        total = jnp.where(row == k, value, total)
    return total


def split(value):
    high = value.astype(bf16)
    return high, (value - high.astype(f32)).astype(bf16)


def kernel(
    nx, ny, levels, rows, cols,
    steps, rate_x, rate_y, gains,
    inc_hbm, dev_hbm, sea_hbm,
    out,
    txh, txl, fx, rx, wy, fy, ry, coef_x, coef_y,
    field, inside, closing_x, end_x, got_x, end_y, got_y, pass_y, chain_y, dev, sea,
    sx_sem, rx_sem, sp_sem, rp_sem, sc_sem, rc_sem, in_sem,
):
    gx, gy = lax.axis_index("gx"), lax.axis_index("gy")
    nb = rows // BX
    half = ny // 2
    inner, outer = lax.rem(gy, 2), gy // 2
    partner = gy + 1 - 2 * inner

    def advance(state, coef, l, index):
        copies = state.shape[1] // 128
        total = None
        for j in range(4):
            scale = jnp.concatenate([coef[l, 4 * index + j]] * copies, 1)
            term = scale * (pltpu.roll(state, j, 0) if j else state)
            total = term if total is None else total + term
        return total

    def three(state):
        high = state.astype(bf16).astype(f32)
        return jnp.concatenate([high, state - high, high, jnp.zeros_like(high)], 0).astype(bf16)

    def dot(a, b, ca=1, cb=0):
        return lax.dot_general(a, b, (((ca,), (cb,)), ((), ())), preferred_element_type=f32)

    def x_copy(l, stage, d, backward):
        target = gx - d if backward else gx + d
        return pltpu.make_async_remote_copy(
            src_ref=end_x.at[stage, l, pl.ds(0, 4)],
            dst_ref=got_x.at[stage, l, d - 1, pl.ds(0, 4)],
            send_sem=sx_sem.at[stage, l, d - 1],
            recv_sem=rx_sem.at[stage, l, d - 1],
            device_id=(target, gy),
            device_id_type=MESH,
        )

    def p_copy(l, stage):
        return pltpu.make_async_remote_copy(
            src_ref=end_y.at[stage, l, pl.ds(0, 4)],
            dst_ref=got_y.at[stage, l, pl.ds(0, 4)],
            send_sem=sp_sem.at[stage, l],
            recv_sem=rp_sem.at[stage, l],
            device_id=(gx, partner),
            device_id_type=MESH,
        )

    def c_copy(l, stage, d, backward):
        target = gy - 2 * d if backward else gy + 2 * d
        return pltpu.make_async_remote_copy(
            src_ref=pass_y.at[stage, l, pl.ds(0, 4)],
            dst_ref=chain_y.at[stage, l, d - 1, pl.ds(0, 4)],
            send_sem=sc_sem.at[stage, l, d - 1],
            recv_sem=rc_sem.at[stage, l, d - 1],
            device_id=(gx, target),
            device_id_type=MESH,
        )

    def x_sends(d, backward):
        return gx >= d if backward else gx + d < nx

    def x_gets(d, backward):
        return gx + d < nx if backward else gx >= d

    def c_sends(d, backward):
        return outer >= d if backward else outer + d < half

    def c_gets(d, backward):
        return outer + d < half if backward else outer >= d

    def start_x(l, value, rep, backward):
        back = int(backward)
        stage = 2 * rep + back
        wide = jnp.concatenate([value[b * BX:(b + 1) * BX] for b in range(nb)], 1)
        high, low = split(wide)
        both = dot(fx[back, l], high) + dot(fx[back, l], low)
        closing = both[:8] + both[8:]
        closing_x[l] = closing
        order = range(nb - 1, -1, -1) if backward else range(nb)
        end = None
        for b in order:
            piece = closing[:, b * cols:(b + 1) * cols]
            end = piece if end is None else advance(end, coef_x, l, 0) + piece
        end_x[stage, l] = end
        for d in range(1, nx):
            @pl.when(x_sends(d, backward))
            def _():
                x_copy(l, stage, d, backward).start()
        for b in range(nb):
            field[l, b * BX:(b + 1) * BX] = value[b * BX:(b + 1) * BX]

    def middle_x(l, backward):
        back = int(backward)
        wide = jnp.concatenate([field[l, b * BX:(b + 1) * BX] for b in range(nb)], 1)
        high, low = split(wide)
        th = txh[back, l]
        inside[l] = dot(th, high) + dot(th, low) + dot(txl[back, l], high)

    def fin_x(l, rep, backward):
        back = int(backward)
        stage = 2 * rep + back
        for d in range(1, nx):
            @pl.when(x_gets(d, backward))
            def _():
                x_copy(l, stage, d, backward).wait_recv()
        carry = got_x[stage, l, 0]
        for d in range(2, nx):
            carry += advance(got_x[stage, l, d - 1], coef_x, l, d - 1)
        order = list(range(nb - 1, -1, -1) if backward else range(nb))
        starts = [None] * nb
        for n, b in enumerate(order):
            starts[b] = carry
            if n < nb - 1:
                carry = advance(carry, coef_x, l, 0) + closing_x[l, :, b * cols:(b + 1) * cols]
        wide = inside[l] + dot(rx[back, l], three(jnp.concatenate(starts, 1)), 0, 0)
        value = jnp.concatenate([wide[:, b * cols:(b + 1) * cols] for b in range(nb)], 0)
        return value * sea[l].astype(f32)

    def start_y(l, value, rep, backward):
        back = int(backward)
        stage = 2 * rep + back
        high, low = split(value)
        pair = jnp.concatenate([high, low], 1)
        ends = jnp.concatenate([fy[back, l]] * 2, 1)
        both = dot(ends, pair, 1, 1)
        end_y[stage, l] = both[:8] + both[8:]
        p_copy(l, stage).start()
        field[l] = value

    def middle_y(l, backward):
        back = int(backward)
        pair = jnp.concatenate(split(field[l]), 1)
        wide = dot(pair, wy[back, l])
        field[l] = wide[:, :cols] + wide[:, cols:]

    def relay_y(l, rep, backward):
        back = int(backward)
        stage = 2 * rep + back
        p_copy(l, stage).wait_recv()
        own, other = end_y[stage, l], got_y[stage, l]
        is_first = inner == (1 if backward else 0)
        first = jnp.where(is_first, own, other)
        second = jnp.where(is_first, other, own)
        pass_y[stage, l] = advance(first, coef_y, l, 0) + second
        for d in range(1, half):
            @pl.when(c_sends(d, backward))
            def _():
                c_copy(l, stage, d, backward).start()

    def fin_y(l, rep, backward):
        back = int(backward)
        stage = 2 * rep + back
        for d in range(1, half):
            @pl.when(c_gets(d, backward))
            def _():
                c_copy(l, stage, d, backward).wait_recv()
        come = chain_y[stage, l, 0]
        for d in range(2, half):
            come += advance(chain_y[stage, l, d - 1], coef_y, l, d - 1)
        is_first = inner == (1 if backward else 0)
        carry = jnp.where(is_first, come, advance(come, coef_y, l, 0) + got_y[stage, l])
        value = field[l] + dot(three(carry), ry[back, l], 0, 0)
        return value * sea[l].astype(f32)

    def each(body):
        lax.fori_loop(0, levels, lambda l, c: (body(l), c)[1], 0, unroll=UNROLL)

    incoming = [
        pltpu.make_async_copy(src, dst, in_sem.at[n])
        for n, (src, dst) in enumerate(((inc_hbm, field), (dev_hbm, dev), (sea_hbm, sea)))
    ]
    for copy in incoming:
        copy.start()
    side = 128
    lags = (
        lax.broadcasted_iota(jnp.int32, (side, side), 0) - lax.broadcasted_iota(jnp.int32, (side, side), 1)
    ).astype(f32)

    def shape_of(lag):
        span = jnp.maximum(lag, 0.0)
        return span, jnp.where(lag > -0.5, (span + 1.0) * (span + 2.0) * (span + 3.0) / 6.0, 0.0)

    near = (shape_of(lags), shape_of(-lags))
    far = (shape_of(side + lags), shape_of(side - lags))

    def tile(shape, rate, weight4):
        return split(weight4 * shape[1] * jnp.exp(-rate * shape[0]))

    def ends(fin, res, l, size, rate, weight):
        row = lax.broadcasted_iota(jnp.int32, (8, size), 0)
        lane = lax.broadcasted_iota(jnp.int32, (8, size), 1).astype(f32)
        pw = [jnp.full((8, size), v) for v in (1.0, weight, weight * weight, weight * weight * weight)]
        for back in (0, 1):
            places = size - 1.0 - lane if back else lane
            remain, ahead = size - places, places + 1.0
            leave, come = binomials(remain), binomials(ahead)
            final = by_row([weight * pw[k] * leave[k] for k in range(4)], row) * jnp.exp(-rate * (remain - 1.0))
            high = final.astype(bf16).astype(f32)
            fin[back, l] = jnp.concatenate([high, final - high], 0).astype(bf16)
            answer = by_row([pw[3 - k] * come[3 - k] for k in range(4)], row) * jnp.exp(-rate * ahead)
            high = answer.astype(bf16).astype(f32)
            res[back, l] = jnp.concatenate(
                [high, high, answer - high, jnp.zeros_like(high)], 0
            ).astype(bf16)

    def coefs(coef, l, spans, rate, weight):
        row = lax.broadcasted_iota(jnp.int32, (8, 128), 0)
        power = (1.0, weight, weight * weight, weight * weight * weight)
        for n, span in enumerate(spans):
            fall = jnp.where(row < 4, jnp.exp(jnp.full((8, 128), -rate * span)), 0.0)
            count = (1.0, span, span * (span + 1.0) / 2.0, span * (span + 1.0) * (span + 2.0) / 6.0)
            for j in range(4):
                coef[l, 4 * n + j] = fall * (power[j] * count[j])

    def build(l):
        rate, weight = rate_x[l], gains[0, l]
        weight4 = weight * weight * weight * weight
        zero = jnp.zeros((side, side), bf16)
        lower, upper = pl.ds(0, side), pl.ds(side, side)
        for back in (0, 1):
            one, two = tile(near[back], rate, weight4), tile(far[back], rate, weight4)
            for ref, close, distant in ((txh, one[0], two[0]), (txl, one[1], two[1])):
                ref[back, l, lower, lower] = close
                ref[back, l, upper, upper] = close
                ref[back, l, lower, upper] = distant if back else zero
                ref[back, l, upper, lower] = zero if back else distant
        ends(fx, rx, l, BX, rate, weight)
        coefs(coef_x, l, [float(BX)] + [float(rows * d) for d in range(1, nx - 1)], rate, weight)
        rate, weight = rate_y[l], gains[1, l]
        weight4 = weight * weight * weight * weight
        for back in (0, 1):
            high, low = tile(near[1 - back], rate, weight4)
            wy[back, l, lower, lower] = high
            wy[back, l, upper, lower] = high
            wy[back, l, lower, upper] = low
            wy[back, l, upper, upper] = zero
        ends(fy, ry, l, cols, rate, weight)
        coefs(coef_y, l, [float(cols)] + [2.0 * cols * d for d in range(1, half - 1)], rate, weight)

    got_x[...] = jnp.zeros_like(got_x)
    got_y[...] = jnp.zeros_like(got_y)
    chain_y[...] = jnp.zeros_like(chain_y)
    barrier = pltpu.get_barrier_semaphore()
    for d in range(1, nx):
        pl.semaphore_signal(barrier, inc=1, device_id=(lax.rem(gx + d, nx), gy), device_id_type=MESH)
    pl.semaphore_signal(barrier, inc=1, device_id=(gx, partner), device_id_type=MESH)
    for d in range(1, half):
        pl.semaphore_signal(barrier, inc=1, device_id=(gx, lax.rem(gy + 2 * d, ny)), device_id_type=MESH)
    lax.fori_loop(0, levels, lambda l, c: (build(l), c)[1], 0)
    pl.semaphore_wait(barrier, nx + half - 1)

    for copy in incoming:
        copy.wait()

    def begin(l):
        value = dev[l] * sea[l].astype(f32) * field[l]
        out[l] = jnp.zeros_like(value)
        start_x(l, value, 0, False)

    each(begin)

    def finish(l, rep):
        value = fin_y(l, rep, True)
        share = jnp.clip((steps[l] - rep).astype(f32), 0.0, 1.0)
        out[l] = share * (dev[l] * value) + (1.0 - share) * out[l]
        return value

    def repetition(rep, c):
        def pairs(l, backward):
            relay_y(l, rep, backward)
            middle_y(l, backward)

        each(lambda l: middle_x(l, False))
        each(lambda l: start_x(l, fin_x(l, rep, False), rep, True))
        each(lambda l: middle_x(l, True))
        each(lambda l: start_y(l, fin_x(l, rep, True), rep, False))
        each(lambda l: pairs(l, False))
        each(lambda l: start_y(l, fin_y(l, rep, False), rep, True))
        each(lambda l: pairs(l, True))

        @pl.when(rep < MAXSTEPS - 1)
        def _():
            each(lambda l: start_x(l, finish(l, rep), rep + 1, False))

        @pl.when(rep == MAXSTEPS - 1)
        def _():
            each(lambda l: (finish(l, rep), None)[1])

        return c

    lax.fori_loop(0, MAXSTEPS, repetition, 0)

    def drain(l):
        for rep in range(MAXSTEPS):
            for backward in (False, True):
                stage = 2 * rep + int(backward)
                for d in range(1, nx):
                    @pl.when(x_sends(d, backward))
                    def _():
                        x_copy(l, stage, d, backward).wait_send()
                p_copy(l, stage).wait_send()

                for d in range(1, half):
                    @pl.when(c_sends(d, backward))
                    def _():
                        c_copy(l, stage, d, backward).wait_send()

    lax.fori_loop(0, levels, lambda l, c: (drain(l), c)[1], 0)


def on_device(nx, ny, increment, deviation, land_sea, filter_steps, zonal_rate, meridional_rate):
    levels, rows, cols = increment.shape
    nb = rows // BX
    gains = section_gain(jnp.stack([zonal_rate, meridional_rate]), filter_steps[None])
    smem = pl.BlockSpec(memory_space=pltpu.SMEM)
    hbm = pl.BlockSpec(memory_space=pltpu.HBM)
    vmem = pl.BlockSpec(memory_space=pltpu.VMEM)
    stages = 2 * MAXSTEPS
    dma = pltpu.SemaphoreType.DMA
    return pl.pallas_call(
        functools.partial(kernel, nx, ny, levels, rows, cols),
        out_shape=jax.ShapeDtypeStruct(increment.shape, f32),
        in_specs=[smem] * 4 + [hbm] * 3,
        out_specs=vmem,
        scratch_shapes=[
            pltpu.VMEM((2, levels, BX, BX), bf16),
            pltpu.VMEM((2, levels, BX, BX), bf16),
            pltpu.VMEM((2, levels, 16, BX), bf16),
            pltpu.VMEM((2, levels, 32, BX), bf16),
            pltpu.VMEM((2, levels, 2 * cols, 2 * cols), bf16),
            pltpu.VMEM((2, levels, 16, cols), bf16),
            pltpu.VMEM((2, levels, 32, cols), bf16),
            pltpu.VMEM((levels, 4 * (nx - 1), 8, 128), f32),
            pltpu.VMEM((levels, 4 * (ny // 2 - 1), 8, 128), f32),
            pltpu.VMEM((levels, rows, cols), f32),
            pltpu.VMEM((levels, BX, nb * cols), f32),
            pltpu.VMEM((levels, 8, nb * cols), f32),
            pltpu.VMEM((stages, levels, 8, cols), f32),
            pltpu.VMEM((stages, levels, nx - 1, 8, cols), f32),
            pltpu.VMEM((stages, levels, 8, rows), f32),
            pltpu.VMEM((stages, levels, 8, rows), f32),
            pltpu.VMEM((stages, levels, 8, rows), f32),
            pltpu.VMEM((stages, levels, ny // 2 - 1, 8, rows), f32),
            pltpu.VMEM((levels, rows, cols), f32),
            pltpu.VMEM((levels, rows, cols), jnp.int32),
            dma((stages, levels, nx - 1)),
            dma((stages, levels, nx - 1)),
            dma((stages, levels)),
            dma((stages, levels)),
            dma((stages, levels, ny // 2 - 1)),
            dma((stages, levels, ny // 2 - 1)),
            dma((3,)),
        ],
        compiler_params=pltpu.CompilerParams(
            collective_id=0, has_side_effects=True, vmem_limit_bytes=40 * 1024 * 1024
        ),
    )(filter_steps, zonal_rate, meridional_rate, gains, increment, deviation, land_sea)


def solution(mesh):
    placed = (P(None, "gx", "gy"), P(None, "gx", "gy"), P(None, "gx", "gy"), P(), P(), P())
    body = functools.partial(on_device, mesh.shape["gx"], mesh.shape["gy"])
    return jax.shard_map(
        body, mesh=mesh, in_specs=placed, out_specs=P(None, "gx", "gy"), check_vma=False
    )
```

profile of v0, /device:TPU:0, one launch (start us, length us, event | category | flops | bytes accessed | tf_op | source)
XLA Modules:
  0.0 72.2 jit_solution(18021502703788106103)
XLA Ops:
  0.0 0.7 divide_subtract_fusion
  0.7 0.7 fusion.3.gains
  1.4 0.0 copy-start
  1.4 1.6 %copy-done = f32[8,512,128]{2,1,0:T(8,128)S(1)} copy-done((f32[8,512,128]{2,1,0:T(8,128)S(1)}, f32[8,512,128]{2,1,0:T(8,128)}, u32[]{:S(2)}) %copy-start) | copy-done | bytes 2097176
  3.0 0.0 copy-start.1
  3.0 1.6 %copy-done.1 = f32[8,512,128]{2,1,0:T(8,128)S(1)} copy-done((f32[8,512,128]{2,1,0:T(8,128)S(1)}, f32[8,512,128]{2,1,0:T(8,128)}, u32[]{:S(2)}) %copy-start.1) | copy-done | bytes 2097176
  4.6 0.0 copy-start.2
  4.6 1.6 %copy-done.2 = s32[8,512,128]{2,1,0:T(8,128)S(1)} copy-done((s32[8,512,128]{2,1,0:T(8,128)S(1)}, s32[8,512,128]{2,1,0:T(8,128)}, u32[]{:S(2)}) %copy-start.2) | copy-done | bytes 2097176
  6.2 0.0 copy-start.3
  6.2 0.7 copy-done.3
  6.8 0.0 copy-start.4
  6.8 0.7 copy-done.4
  7.5 0.0 copy-start.5
  7.5 0.7 copy-done.5
  8.1 62.8 %shard_map.64 = f32[8,512,128]{2,1,0:T(8,128)S(1)} custom-call(s32[8]{0:T(128)S(1)} %copy-done.5, f32[8]{0:T(128)S(1)} %copy-done.3, f32[8]{0:T(128)S(1)} %copy-done.4, f32[2,8]{1,0:T(2,128)S(1)} %fusion.3.gains, f32[8,512,128]{2,1,0:T(8,128)S(1)} %copy-done, f32[8,512,128]{2,1,0:T(8,128)S(1)} %copy-done.1, s32[8,512,128]{2,1,0:T(8,128)S(1)} %copy-done.2), custom_call_target="tpu_custom_call" | custom-call | tf_op jit(solution)/shard_map/pallas_call | solution.py:368
  70.9 1.3 %copy.8 = f32[8,512,128]{2,1,0:T(8,128)} copy(f32[8,512,128]{2,1,0:T(8,128)S(1)} %shard_map.64) | data formatting | bytes 4194304
Async XLA Ops:
  1.4 1.6 %copy-start = (f32[8,512,128]{2,1,0:T(8,128)S(1)}, f32[8,512,128]{2,1,0:T(8,128)}, u32[]{:S(2)}) copy-start(f32[8,512,128]{2,1,0:T(8,128)} %inc_hbm.1) | copy-start | bytes 6291460
  3.0 1.6 %copy-start.1 = (f32[8,512,128]{2,1,0:T(8,128)S(1)}, f32[8,512,128]{2,1,0:T(8,128)}, u32[]{:S(2)}) copy-start(f32[8,512,128]{2,1,0:T(8,128)} %dev_hbm.1) | copy-start | bytes 6291460
  4.6 1.6 %copy-start.2 = (s32[8,512,128]{2,1,0:T(8,128)S(1)}, s32[8,512,128]{2,1,0:T(8,128)}, u32[]{:S(2)}) copy-start(s32[8,512,128]{2,1,0:T(8,128)} %sea_hbm.1) | copy-start | bytes 6291460
  6.2 0.7 copy-start.3
  6.8 0.7 copy-start.4
  7.5 0.7 copy-start.5
where the time goes:
time: 72.5 us; the launch traced here: 72.2 us
  Pallas kernels  62.8 us (87%)
  local copies, waits for them, and re-layouts  8.05 us (11%)
  other arithmetic  1.37 us (2%)
    pallas_call x1, Pallas kernels, on_device(): pl.pallas_call(functools.partial(kernel, nx, ny, levels, rows, cols), out...  62.8 us
    unnamed x13, local copies, waits for them, and re-layouts  8.05 us

commit v1 on v0

v1 whole, which is shorter than its diff:
```python
import functools

import jax
import jax.numpy as jnp
from jax import lax
from jax.experimental import pallas as pl
from jax.experimental.pallas import tpu as pltpu
from jax.sharding import PartitionSpec as P

SIDE = 128
PAIR = 2
MAXSTEPS = 2
gain_base = 3.0**0.125
MESH = pl.DeviceIdType.MESH
f32, bf16 = jnp.float32, jnp.bfloat16


def section_gain(decay_rate, filter_steps):
    fading = -jnp.expm1(-decay_rate)
    return gain_base * fading ** (1.0 - 1.0 / (16.0 * filter_steps.astype(f32)))


def binomials(count):
    return (
        jnp.ones_like(count),
        count,
        count * (count + 1.0) / 2.0,
        count * (count + 1.0) * (count + 2.0) / 6.0,
    )


def split(value):
    high = value.astype(bf16)
    return high, (value - high.astype(f32)).astype(bf16)


def three(state):
    high = state.astype(bf16).astype(f32)
    return jnp.concatenate([high, state - high, high, jnp.zeros_like(high)], 0).astype(bf16)


def dot(a, b, ca=1, cb=0):
    return lax.dot_general(a, b, (((ca,), (cb,)), ((), ())), preferred_element_type=f32)


def kernel(
    nx, ny, levels, rows, cols,
    steps, rate_x, rate_y, gains,
    inc_hbm, dev_hbm, sea_hbm,
    out,
    wx, rx, wy, fy, ry, tx, ty, coef_x, coef_y,
    inside, before, ends_x, block_x, mix_x, mix_y, got_m,
    end_x, got_x, end_y, got_y, back_y, come_y, inc, dev, sea, wet,
    smx, rmx, smy, rmy, sx, rx_sem, sy, ry_sem, sb, rb, in_sem,
):
    gx, gy = lax.axis_index("gx"), lax.axis_index("gy")
    nb = rows // SIDE
    groups = levels // PAIR
    share = rows // ny
    mid = 64
    row = lax.broadcasted_iota(jnp.int32, (8, 128), 0)
    lane = lax.broadcasted_iota(jnp.int32, (8, 128), 1)
    place = jnp.where(row < 4, row, row - 4)
    left = lane < mid

    def turned(state):
        return [state] + [pltpu.roll(state, j, 0) for j in range(1, 4)]

    def advance(turns, coef, g, index):
        total = None
        for j in range(4):
            term = coef[g, 4 * index + j] * turns[j]
            total = term if total is None else total + term
        return total

    def mixed(mix, turns):
        total = mix[0] * turns[0]
        for j in range(1, 4):
            total += mix[j] * jnp.where(place >= j, turns[j], pltpu.roll(turns[0], j + 4, 0))
        return total

    def slide(tile, count):
        count = count % 128
        return pltpu.roll(tile, count, 1) if count else tile

    def x_peer(d):
        return (lax.rem(gx + d, nx), gy)

    def y_peer(d):
        return (gx, lax.rem(gy + d, ny))

    def mx_copy(g, d):
        return pltpu.make_async_remote_copy(
            src_ref=mix_x.at[g, gx], dst_ref=mix_x.at[g, gx],
            send_sem=smx.at[d - 1], recv_sem=rmx.at[g],
            device_id=x_peer(d), device_id_type=MESH,
        )

    def my_copy(g, d):
        return pltpu.make_async_remote_copy(
            src_ref=mix_y.at[g, lax.rem(gy + d, ny)], dst_ref=got_m.at[g, gy],
            send_sem=smy.at[d - 1], recv_sem=rmy.at[g],
            device_id=y_peer(d), device_id_type=MESH,
        )

    def x_copy(g, rep, d):
        return pltpu.make_async_remote_copy(
            src_ref=end_x.at[rep, g], dst_ref=got_x.at[rep, g, gx],
            send_sem=sx.at[rep, d - 1], recv_sem=rx_sem.at[rep, g],
            device_id=x_peer(d), device_id_type=MESH,
        )

    def y_copy(g, rep, d):
        return pltpu.make_async_remote_copy(
            src_ref=end_y.at[rep, g, lax.rem(gy + d, ny)], dst_ref=got_y.at[rep, g, gy],
            send_sem=sy.at[rep, d - 1], recv_sem=ry_sem.at[rep, g],
            device_id=y_peer(d), device_id_type=MESH,
        )

    def b_copy(g, rep, d):
        return pltpu.make_async_remote_copy(
            src_ref=back_y.at[rep, g, lax.rem(gy + d, ny)], dst_ref=come_y.at[rep, g, gy],
            send_sem=sb.at[rep, d - 1], recv_sem=rb.at[rep, g],
            device_id=y_peer(d), device_id_type=MESH,
        )

    def taken(ref, sem):
        pltpu.make_async_copy(ref, ref, sem).wait()

    def blocks(value):
        return jnp.concatenate([value[b * SIDE:(b + 1) * SIDE] for b in range(nb)], 1)

    def unblock(wide):
        return jnp.concatenate([wide[:, b * cols:(b + 1) * cols] for b in range(nb)], 0)

    def stack(value):
        return jnp.concatenate(split(value), 0)

    def halves(both):
        return both[:8] + both[8:16]

    def tiles(wide):
        return [wide[:, t * 128:(t + 1) * 128] for t in range(wide.shape[1] // 128)]

    def plus(total, piece):
        return piece if total is None else total + piece

    def packed(first, second, k):
        t, off = (k * share) // 128, (k * share) % 128
        return jnp.where(left, slide(first[t], -off), slide(second[t], mid - off))

    def x_first(g, values, rep):
        closing = opening = None
        for i, value in enumerate(values):
            l = PAIR * g + i
            both = dot(wx[0, l], stack(blocks(value)))
            held = both[:SIDE] + both[SIDE:2 * SIDE]
            inside[l] = held
            closing = plus(closing, halves(both[2 * SIDE:]))
            masked = stack(held * blocks(wet[l]))
            opening = plus(opening, halves(dot(wx[1, l, pl.ds(2 * SIDE, 16), :], masked)))
        closing, opening = tiles(closing), tiles(opening)
        carry = closing[0]
        chain = [opening[0]]
        ends_x[g, 0] = opening[0]
        for n in range(1, nb):
            turns = turned(carry)
            before[g, n - 1] = carry
            ends_x[g, n] = opening[n]
            chain.append(opening[n] + mixed([block_x[g, j, :, pl.ds(n * 128, 128)] for j in range(4)], turns))
            carry = advance(turns, coef_x, g, 0) + closing[n]
        end = chain[-1]
        for n in range(nb - 2, -1, -1):
            end = advance(turned(end), coef_x, g, 0) + chain[n]
        message = jnp.concatenate([carry, end], 0)
        end_x[rep, g] = message
        got_x[rep, g, gx] = message
        for d in range(1, nx):
            x_copy(g, rep, d).start()

    def x_second(g, rep):
        taken(got_x.at[rep, g, pl.ds(0, nx - 1)], rx_sem.at[rep, g])
        carry = got_x[rep, g, 0, pl.ds(0, 8)]
        zero = jnp.zeros_like(carry)
        come = zero
        ending = [None] * nx
        for j in range(1, nx):
            turns = turned(carry)
            come = jnp.where(gx == j, carry, come)
            ending[j] = got_x[rep, g, j, pl.ds(8, 8)] + mixed(
                [mix_x[g, j, pl.ds(8 * k, 8)] for k in range(4)], turns
            )
            if j < nx - 1:
                carry = advance(turns, coef_x, g, nb - 1) + got_x[rep, g, j, pl.ds(0, 8)]
        carry = ending[nx - 1]
        leave = jnp.where(gx == nx - 2, carry, zero)
        for j in range(nx - 2, 0, -1):
            carry = advance(turned(carry), coef_x, g, nb - 1) + ending[j]
            leave = jnp.where(gx == j - 1, carry, leave)
        turns = turned(come)
        starts = [come] + [advance(turns, coef_x, g, n - 1) + before[g, n - 1] for n in range(1, nb)]
        lasts = [None] * nb
        lasts[nb - 1] = leave
        for n in range(nb - 1, 0, -1):
            ending_n = ends_x[g, n] + mixed(
                [block_x[g, j, :, pl.ds(n * 128, 128)] for j in range(4)], turned(starts[n])
            )
            lasts[n - 1] = advance(turned(lasts[n]), coef_x, g, 0) + ending_n
        ahead, behind = three(jnp.concatenate(starts, 1)), three(jnp.concatenate(lasts, 1))
        values = []
        for i in range(PAIR):
            l = PAIR * g + i
            mask = blocks(wet[l])
            field = (inside[l] + dot(rx[0, l], ahead, 0, 0)) * mask
            both = dot(wx[1, l, pl.ds(0, 2 * SIDE), :], stack(field))
            field = both[:SIDE] + both[SIDE:] + dot(rx[1, l], behind, 0, 0)
            values.append(unblock(field * mask))
        return values

    def y_first(g, values, rep):
        closing = opening = None
        for i, value in enumerate(values):
            l = PAIR * g + i
            pair = jnp.concatenate(split(value), 1)
            closing = plus(closing, halves(dot(fy[0, l], pair, 1, 1)))
            wide = dot(pair, wy[0, l])
            held = wide[:, :cols] + wide[:, cols:]
            inside[l] = blocks(held)
            pair = jnp.concatenate(split(held * wet[l]), 1)
            opening = plus(opening, halves(dot(fy[1, l], pair, 1, 1)))
        closing, opening = tiles(closing), tiles(opening)
        for k in range(ny):
            end_y[rep, g, k] = packed(closing, opening, k)
        got_y[rep, g, gy] = end_y[rep, g, gy]
        for d in range(1, ny):
            y_copy(g, rep, d).start()

    def y_owner(g, rep):
        taken(got_y.at[rep, g, pl.ds(0, ny - 1)], ry_sem.at[rep, g])
        got = [got_y[rep, g, j] for j in range(ny)]
        first = [jnp.where(left, tile, slide(tile, mid)) for tile in got]
        starts, ending = [None] * ny, [None] * ny
        starts[0] = jnp.zeros_like(first[0])
        carry = first[0]
        for j in range(1, ny):
            turns = turned(carry)
            starts[j] = carry
            even, odd = got_m[g, j, pl.ds(0, 8)], got_m[g, j, pl.ds(8, 8)]
            ending[j] = got[j] + mixed([slide(even, mid), even, slide(odd, mid), odd], turns)
            if j < ny - 1:
                carry = advance(turns, coef_y, g, 0) + first[j]
        last = jnp.zeros_like(carry)
        for j in range(ny - 1, -1, -1):
            back_y[rep, g, j] = jnp.where(left, starts[j], last)
            if j:
                last = ending[j] if j == ny - 1 else advance(turned(last), coef_y, g, 0) + ending[j]
        come_y[rep, g, gy] = back_y[rep, g, gy]
        for d in range(1, ny):
            b_copy(g, rep, d).start()

    def y_second(g, rep):
        taken(come_y.at[rep, g, pl.ds(0, ny - 1)], rb.at[rep, g])
        starts, lasts = [None] * (rows // 128), [None] * (rows // 128)
        for k in range(ny):
            t, off = (k * share) // 128, (k * share) % 128
            tile = come_y[rep, g, k]
            start, last = slide(tile, off), slide(tile, off - mid)
            if off == 0:
                starts[t], lasts[t] = start, last
            else:
                starts[t] = jnp.where(lane >= off, start, starts[t])
                lasts[t] = jnp.where(lane >= off, last, lasts[t])
        ahead = dot(three(jnp.concatenate(starts, 1)), ry[0, g], 0, 0)
        behind = dot(three(jnp.concatenate(lasts, 1)), ry[1, g], 0, 0)
        values = []
        for i in range(PAIR):
            l = PAIR * g + i
            own = slice(i * cols, (i + 1) * cols)
            mask = wet[l]
            field = (unblock(inside[l]) + ahead[:, own]) * mask
            wide = dot(jnp.concatenate(split(field), 1), wy[1, l])
            values.append((wide[:, :cols] + wide[:, cols:] + behind[:, own]) * mask)
        return values

    def each(body, unroll=1):
        lax.fori_loop(0, groups, lambda g, c: (body(g), c)[1], 0, unroll=unroll)

    sources = ((sea_hbm, sea), (inc_hbm, inc), (dev_hbm, dev))

    def incoming(l, n):
        src, dst = sources[n]
        return pltpu.make_async_copy(src.at[l], dst.at[l], in_sem.at[n, l])

    for l in range(levels):
        for n in range(3):
            incoming(l, n).start()

    lags = (
        lax.broadcasted_iota(jnp.int32, (SIDE, SIDE), 0) - lax.broadcasted_iota(jnp.int32, (SIDE, SIDE), 1)
    ).astype(f32)

    def shape_of(lag):
        span = jnp.maximum(lag, 0.0)
        return span, jnp.where(lag > -0.5, (span + 1.0) * (span + 2.0) * (span + 3.0) / 6.0, 0.0)

    near = (shape_of(lags), shape_of(-lags))

    def tile(shape, rate, weight):
        weight4 = weight * weight * weight * weight
        return split(weight4 * shape[1] * jnp.exp(-rate * shape[0]))

    def by_row(values, i):
        total = jnp.zeros(row.shape, f32)
        for k, value in enumerate(values):
            total = jnp.where(row == k + 4 * i, value, total)
        return total

    def powers(weight):
        return [jnp.full((8, 128), v) for v in (1.0, weight, weight * weight, weight * weight * weight)]

    def final_of(i, places, rate, weight):
        pw, leave = powers(weight), binomials(places + 1.0)
        return by_row([weight * pw[k] * leave[k] for k in range(4)], i) * jnp.exp(-rate * places)

    def answer_of(i, places, rate, weight):
        pw, ahead = powers(weight), places + 1.0
        come = binomials(ahead)
        return by_row([pw[3 - k] * come[3 - k] for k in range(4)], i) * jnp.exp(-rate * ahead)

    def high_low(value):
        high = value.astype(bf16).astype(f32)
        return high, value - high

    def ends(i, back, rate, weight):
        across = lane.astype(f32)
        mirror = SIDE - 1.0 - across
        high, low = high_low(final_of(i, across if back else mirror, rate, weight))
        finals = jnp.concatenate([high, low], 0).astype(bf16)
        high, low = high_low(answer_of(i, mirror if back else across, rate, weight))
        answers = jnp.concatenate([high, high, low, jnp.zeros_like(high)], 0).astype(bf16)
        return finals, answers

    def products(i, places, rate, weight):
        final = final_of(i, places, rate, weight)
        turns = turned(answer_of(i, places, rate, weight))
        parts = []
        for j in range(4):
            turn = turns[0] if j == 0 else jnp.where(place >= j, turns[j], pltpu.roll(turns[0], j + 4, 0))
            parts += list(high_low(final * turn))
        return jnp.concatenate(parts, 0).astype(bf16)

    def coefs(coef, g, spans, rates, weights):
        low = row < 4
        rate = jnp.where(low, rates[0], rates[1])
        weight = jnp.where(low, weights[0], weights[1])
        power = (jnp.ones_like(weight), weight, weight * weight, weight * weight * weight)
        for n, span in enumerate(spans):
            fall = jnp.exp(-rate * span)
            count = (1.0, span, span * (span + 1.0) / 2.0, span * (span + 1.0) * (span + 2.0) / 6.0)
            for j in range(4):
                coef[g, 4 * n + j] = jnp.where(place >= j, fall * (power[j] * count[j]), 0.0)

    def build(g):
        zero = jnp.zeros((SIDE, SIDE), bf16)
        across = lane.astype(f32)
        lower, upper, rest = pl.ds(0, SIDE), pl.ds(SIDE, SIDE), pl.ds(2 * SIDE, 16)
        for i in range(PAIR):
            l = PAIR * g + i
            rate, weight = rate_x[l], gains[0, l]
            for back in (0, 1):
                high, low = tile(near[back], rate, weight)
                wx[back, l, lower, lower] = high
                wx[back, l, lower, upper] = high
                wx[back, l, upper, lower] = low
                wx[back, l, upper, upper] = zero
                finals, answers = ends(i, back, rate, weight)
                wx[back, l, rest, lower] = finals
                wx[back, l, rest, upper] = finals
                rx[back, l] = answers
            for b in range(nb):
                tx[l, :, pl.ds(b * SIDE, SIDE)] = products(i, across + float(b * SIDE), rate, weight)
            rate, weight = rate_y[l], gains[1, l]
            for back in (0, 1):
                high, low = tile(near[1 - back], rate, weight)
                wy[back, l, lower, lower] = high
                wy[back, l, upper, lower] = high
                wy[back, l, lower, upper] = low
                wy[back, l, upper, upper] = zero
                finals, answers = ends(i, back, rate, weight)
                fy[back, l, :, lower] = finals
                fy[back, l, :, upper] = finals
                ry[back, g, :, pl.ds(i * cols, cols)] = answers
            ty[l] = products(i, across, rate, weight)
        two = [PAIR * g + i for i in range(PAIR)]
        spans = [float(SIDE * n) for n in range(1, nb)] + [float(rows)]
        coefs(coef_x, g, spans, [rate_x[l] for l in two], [gains[0, l] for l in two])
        coefs(coef_y, g, [float(cols)], [rate_y[l] for l in two], [gains[1, l] for l in two])

    barrier = pltpu.get_barrier_semaphore()
    for d in range(1, nx):
        pl.semaphore_signal(barrier, inc=1, device_id=x_peer(d), device_id_type=MESH)
    for d in range(1, ny):
        pl.semaphore_signal(barrier, inc=1, device_id=y_peer(d), device_id_type=MESH)

    each(build)
    pl.semaphore_wait(barrier, nx + ny - 2)

    def four(wide):
        return [halves(wide[16 * j:16 * j + 16]) for j in range(4)]

    def begin(g):
        values = []
        device = block = across = None
        for i in range(PAIR):
            l = PAIR * g + i
            incoming(l, 0).wait()
            mask = sea[l].astype(f32)
            wet[l] = mask
            mask = mask.astype(bf16)
            device = plus(device, dot(tx[l], mask))
            block = plus(block, dot(tx[l, :, pl.ds(0, SIDE)], blocks(mask)))
            across = plus(across, dot(ty[l], mask, 1, 1))
        mix_x[g, gx] = jnp.concatenate(four(device), 0)
        for d in range(1, nx):
            mx_copy(g, d).start()
        for j, part in enumerate(four(block)):
            block_x[g, j] = part
        parts = [tiles(part) for part in four(across)]
        for k in range(ny):
            mix_y[g, k] = jnp.concatenate([packed(parts[0], parts[1], k), packed(parts[2], parts[3], k)], 0)
        got_m[g, gy] = mix_y[g, gy]
        for d in range(1, ny):
            my_copy(g, d).start()
        for i in range(PAIR):
            l = PAIR * g + i
            for n in (1, 2):
                incoming(l, n).wait()
            values.append(dev[l] * wet[l] * inc[l])
        x_first(g, values, 0)

    each(begin)

    def repetition(rep, c):
        @pl.when(rep == 0)
        def _():
            for g in range(groups):
                taken(mix_x.at[g, pl.ds(0, nx - 1)], rmx.at[g])

        each(lambda g: y_first(g, x_second(g, rep), rep))

        @pl.when(rep == 0)
        def _():
            for g in range(groups):
                taken(got_m.at[g, pl.ds(0, ny - 1)], rmy.at[g])

        each(lambda g: y_owner(g, rep))

        @pl.when(rep < MAXSTEPS - 1)
        def _():
            def more(g):
                values = y_second(g, rep)
                for i, value in enumerate(values):
                    out[PAIR * g + i] = dev[PAIR * g + i] * value
                x_first(g, values, rep + 1)

            each(more)

        @pl.when(rep == MAXSTEPS - 1)
        def _():
            def last(g):
                values = y_second(g, rep)
                for i, value in enumerate(values):
                    l = PAIR * g + i
                    out[l] = jnp.where(steps[l] > rep, dev[l] * value, out[l])

            each(last)

        return c

    lax.fori_loop(0, MAXSTEPS, repetition, 0)

    for d in range(1, nx):
        taken(mix_x.at[:, 0], smx.at[d - 1])
        for rep in range(MAXSTEPS):
            taken(end_x.at[rep], sx.at[rep, d - 1])
    for d in range(1, ny):
        taken(mix_y.at[:, 0], smy.at[d - 1])
        for rep in range(MAXSTEPS):
            taken(end_y.at[rep, :, 0], sy.at[rep, d - 1])
            taken(back_y.at[rep, :, 0], sb.at[rep, d - 1])


def on_device(nx, ny, increment, deviation, land_sea, filter_steps, zonal_rate, meridional_rate):
    levels, rows, cols = increment.shape
    nb = rows // SIDE
    groups = levels // PAIR
    gains = section_gain(jnp.stack([zonal_rate, meridional_rate]), filter_steps[None])
    smem = pl.BlockSpec(memory_space=pltpu.SMEM)
    hbm = pl.BlockSpec(memory_space=pltpu.HBM)
    vmem = pl.BlockSpec(memory_space=pltpu.VMEM)
    reps = MAXSTEPS
    dma = pltpu.SemaphoreType.DMA
    return pl.pallas_call(
        functools.partial(kernel, nx, ny, levels, rows, cols),
        out_shape=jax.ShapeDtypeStruct(increment.shape, f32),
        in_specs=[smem] * 4 + [hbm] * 3,
        out_specs=vmem,
        scratch_shapes=[
            pltpu.VMEM((2, levels, 2 * SIDE + 16, 2 * SIDE), bf16),
            pltpu.VMEM((2, levels, 32, SIDE), bf16),
            pltpu.VMEM((2, levels, 2 * cols, 2 * cols), bf16),
            pltpu.VMEM((2, levels, 16, 2 * cols), bf16),
            pltpu.VMEM((2, groups, 32, PAIR * cols), bf16),
            pltpu.VMEM((levels, 64, rows), bf16),
            pltpu.VMEM((levels, 64, cols), bf16),
            pltpu.VMEM((groups, 4 * nb, 8, 128), f32),
            pltpu.VMEM((groups, 4, 8, 128), f32),
            pltpu.VMEM((levels, SIDE, nb * cols), f32),
            pltpu.VMEM((groups, nb - 1, 8, cols), f32),
            pltpu.VMEM((groups, nb, 8, cols), f32),
            pltpu.VMEM((groups, 4, 8, nb * cols), f32),
            pltpu.VMEM((groups, nx, 32, cols), f32),
            pltpu.VMEM((groups, ny, 16, 128), f32),
            pltpu.VMEM((groups, ny, 16, 128), f32),
            pltpu.VMEM((reps, groups, 16, cols), f32),
            pltpu.VMEM((reps, groups, nx, 16, cols), f32),
            pltpu.VMEM((reps, groups, ny, 8, 128), f32),
            pltpu.VMEM((reps, groups, ny, 8, 128), f32),
            pltpu.VMEM((reps, groups, ny, 8, 128), f32),
            pltpu.VMEM((reps, groups, ny, 8, 128), f32),
            pltpu.VMEM((levels, rows, cols), f32),
            pltpu.VMEM((levels, rows, cols), f32),
            pltpu.VMEM((levels, rows, cols), jnp.int32),
            pltpu.VMEM((levels, rows, cols), f32),
            dma((nx - 1,)),
            dma((groups,)),
            dma((ny - 1,)),
            dma((groups,)),
            dma((reps, nx - 1)),
            dma((reps, groups)),
            dma((reps, ny - 1)),
            dma((reps, groups)),
            dma((reps, ny - 1)),
            dma((reps, groups)),
            dma((3, levels)),
        ],
        compiler_params=pltpu.CompilerParams(
            collective_id=0, has_side_effects=True, vmem_limit_bytes=40 * 1024 * 1024
        ),
    )(
        filter_steps, zonal_rate, meridional_rate, gains,
        *(pltpu.with_memory_space_constraint(a, pltpu.HBM) for a in (increment, deviation, land_sea)),
    )


def solution(mesh):
    placed = (P(None, "gx", "gy"), P(None, "gx", "gy"), P(None, "gx", "gy"), P(), P(), P())
    body = functools.partial(on_device, mesh.shape["gx"], mesh.shape["gy"])
    return jax.shard_map(
        body, mesh=mesh, in_specs=placed, out_specs=P(None, "gx", "gy"), check_vma=False
    )
```

time: 72.5 us -> 48.6 us (0.67)
  Pallas kernels: 62.8 us -> 43.7 us
  local copies, waits for them, and re-layouts: 8.05 us -> 3.28 us
    pallas_call x1, Pallas kernels: 62.8 us -> 43.7 us  [on_device(): pl.pallas_call(functools.partial(kernel, nx, ny, levels, rows, cols), out...]
    unnamed x13 -> x7, local copies, waits for them, and re-layouts: 8.05 us -> 3.28 us
where the time goes in v1:
time: 48.6 us; the launch traced here: 48.4 us
  Pallas kernels  43.7 us (90%)
  local copies, waits for them, and re-layouts  3.28 us (7%)
  other arithmetic  1.37 us (3%)
    pallas_call x1, Pallas kernels, on_device(): pl.pallas_call(functools.partial(kernel, nx, ny, levels, rows, cols), out...  43.7 us
    unnamed x7, local copies, waits for them, and re-layouts  3.28 us

profile of v1, /device:TPU:0, one launch (start us, length us, event | category | flops | bytes accessed | tf_op | source)
XLA Modules:
  0.0 48.4 jit_solution(3081325262037008964)
XLA Ops:
  0.0 0.7 %divide_subtract_fusion = f32[8]{0:T(128)S(1)} fusion(s32[8]{0:T(128)} %steps.1), kind=kLoop, calls=%fused_computation.5 | loop fusion | flops 32 | bytes 64 | tf_op jit(solution)/shard_map/sub | solution.py:20
  0.7 0.7 %fusion.3.gains = f32[2,8]{1,0:T(2,128)S(1)} fusion(f32[1,8]{1,0:T(1,128)} %bitcast.3, f32[1,8]{1,0:T(1,128)} %bitcast.2, f32[8]{0:T(128)S(1)} %divide_subtract_fusion), kind=kLoop, calls=%fused_computation.4 | loop fusion | flops 64 | bytes 160 | tf_op jit(solution)/shard_map/mul | solution.py:20
  1.4 0.0 copy-start
  1.4 0.6 %copy-done = f32[8]{0:T(128)S(1)} copy-done((f32[8]{0:T(128)S(1)}, f32[8]{0:T(128)}, u32[]{:S(2)}) %copy-start) | copy-done | bytes 56
  2.0 0.0 copy-start.1
  2.0 0.7 %copy-done.1 = f32[8]{0:T(128)S(1)} copy-done((f32[8]{0:T(128)S(1)}, f32[8]{0:T(128)}, u32[]{:S(2)}) %copy-start.1) | copy-done | bytes 56
  2.7 0.0 copy-start.2
  2.7 0.7 %copy-done.2 = s32[8]{0:T(128)S(1)} copy-done((s32[8]{0:T(128)S(1)}, s32[8]{0:T(128)}, u32[]{:S(2)}) %copy-start.2) | copy-done | bytes 56
  3.3 43.7 %shard_map.64 = f32[8,512,128]{2,1,0:T(8,128)S(1)} custom-call(s32[8]{0:T(128)S(1)} %copy-done.2, f32[8]{0:T(128)S(1)} %copy-done, f32[8]{0:T(128)S(1)} %copy-done.1, f32[2,8]{1,0:T(2,128)S(1)} %fusion.3.gains, f32[8,512,128]{2,1,0:T(8,128)} %inc_hbm.1, f32[8,512,128]{2,1,0:T(8,128)} %dev_hbm.1, s32[8,512,128]{2,1,0:T(8,128)} %sea_hbm.1), custom_call_target="tpu_custom_call" | custom-call | tf_op jit(solution)/shard_map/pallas_call | solution.py:503
  47.1 1.3 %copy.8 = f32[8,512,128]{2,1,0:T(8,128)} copy(f32[8,512,128]{2,1,0:T(8,128)S(1)} %shard_map.64) | data formatting | bytes 4194304
Async XLA Ops:
  1.4 0.7 %copy-start = (f32[8]{0:T(128)S(1)}, f32[8]{0:T(128)}, u32[]{:S(2)}) copy-start(f32[8]{0:T(128)} %rate_x.1) | copy-start | bytes 100
  2.0 0.7 %copy-start.1 = (f32[8]{0:T(128)S(1)}, f32[8]{0:T(128)}, u32[]{:S(2)}) copy-start(f32[8]{0:T(128)} %rate_y.1) | copy-start | bytes 100
  2.7 0.7 %copy-start.2 = (s32[8]{0:T(128)S(1)}, s32[8]{0:T(128)}, u32[]{:S(2)}) copy-start(s32[8]{0:T(128)} %steps.1) | copy-start | bytes 100

commit v2 on v1

v2 whole, which is shorter than its diff:
```python
import functools

import jax
import jax.numpy as jnp
from jax import lax
from jax.experimental import pallas as pl
from jax.experimental.pallas import tpu as pltpu
from jax.sharding import PartitionSpec as P

SIDE = 128
PAIR = 2
TEAM = 2
MAXSTEPS = 2
gain_base = 3.0**0.125
MESH = pl.DeviceIdType.MESH
f32, bf16 = jnp.float32, jnp.bfloat16


def section_gain(decay_rate, filter_steps):
    rate = jnp.full((8, 128), decay_rate)
    count = jnp.full((8, 128), filter_steps.astype(f32))
    series = jnp.ones_like(rate)
    for n in range(9, 1, -1):
        series = 1.0 - series * rate * (1.0 / n)
    fading = jnp.where(rate < 0.5, rate * series, 1.0 - jnp.exp(-rate))
    return gain_base * jnp.exp((1.0 - 1.0 / (16.0 * count)) * jnp.log(fading))


def binomials(count):
    return (
        jnp.ones_like(count),
        count,
        count * (count + 1.0) / 2.0,
        count * (count + 1.0) * (count + 2.0) / 6.0,
    )


def split(value):
    high = value.astype(bf16)
    return high, (value - high.astype(f32)).astype(bf16)


def three(state):
    high = state.astype(bf16).astype(f32)
    return jnp.concatenate([high, state - high, high, jnp.zeros_like(high)], 0).astype(bf16)


def dot(a, b, ca=1, cb=0):
    return lax.dot_general(a, b, (((ca,), (cb,)), ((), ())), preferred_element_type=f32)


def kernel(
    nx, ny, levels, rows, cols,
    steps_hbm, rate_x_hbm, rate_y_hbm,
    inc_hbm, dev_hbm, sea_hbm,
    out,
    steps, rate_x, rate_y,
    wx, bx, rx, wy, by, ry, tx, ty, coef_x, coef_y,
    inside, before, ends_x, block_x, mix_x, mix_y, got_m,
    end_x, got_x, end_y, got_y, back_y, come_y, inc, dev, sea, wet, wet_t, kept,
    smx, rmx, smy, rmy, sx, rx_sem, sy, ry_sem, sb, rb, in_sem, few_sem,
):
    gx, gy = lax.axis_index("gx"), lax.axis_index("gy")
    nb = rows // SIDE
    groups = levels // PAIR
    share = rows // ny
    mid = 64
    row = lax.broadcasted_iota(jnp.int32, (8, 128), 0)
    lane = lax.broadcasted_iota(jnp.int32, (8, 128), 1)
    place = jnp.where(row < 4, row, row - 4)
    left = lane < mid

    def turned(state):
        return [state] + [pltpu.roll(state, j, 0) for j in range(1, 4)]

    def advance(turns, coef, g, index):
        total = None
        for j in range(4):
            term = coef[g, 4 * index + j] * turns[j]
            total = term if total is None else total + term
        return total

    def mixed(mix, turns):
        total = mix[0] * turns[0]
        for j in range(1, 4):
            total += mix[j] * jnp.where(place >= j, turns[j], pltpu.roll(turns[0], j + 4, 0))
        return total

    def slide(tile, count):
        count = count % 128
        return pltpu.roll(tile, count, 1) if count else tile

    def x_peer(d):
        return (lax.rem(gx + d, nx), gy)

    def y_peer(d):
        return (gx, lax.rem(gy + d, ny))

    def mx_copy(g, d):
        return pltpu.make_async_remote_copy(
            src_ref=mix_x.at[g, gx], dst_ref=mix_x.at[g, gx],
            send_sem=smx.at[d - 1], recv_sem=rmx.at[g],
            device_id=x_peer(d), device_id_type=MESH,
        )

    def my_copy(g, d):
        return pltpu.make_async_remote_copy(
            src_ref=mix_y.at[g, lax.rem(gy + d, ny)], dst_ref=got_m.at[g, gy],
            send_sem=smy.at[d - 1], recv_sem=rmy.at[g],
            device_id=y_peer(d), device_id_type=MESH,
        )

    def x_copy(g, rep, d):
        return pltpu.make_async_remote_copy(
            src_ref=end_x.at[rep, g], dst_ref=got_x.at[rep, g, gx],
            send_sem=sx.at[rep, d - 1], recv_sem=rx_sem.at[rep, g],
            device_id=x_peer(d), device_id_type=MESH,
        )

    def y_copy(g, rep, d):
        return pltpu.make_async_remote_copy(
            src_ref=end_y.at[rep, g, lax.rem(gy + d, ny)], dst_ref=got_y.at[rep, g, gy],
            send_sem=sy.at[rep, d - 1], recv_sem=ry_sem.at[rep, g],
            device_id=y_peer(d), device_id_type=MESH,
        )

    def b_copy(g, rep, d):
        return pltpu.make_async_remote_copy(
            src_ref=back_y.at[rep, g, lax.rem(gy + d, ny)], dst_ref=come_y.at[rep, g, gy],
            send_sem=sb.at[rep, d - 1], recv_sem=rb.at[rep, g],
            device_id=y_peer(d), device_id_type=MESH,
        )

    def taken(ref, sem):
        pltpu.make_async_copy(ref, ref, sem).wait()

    def blocks(value):
        return jnp.concatenate([value[b * SIDE:(b + 1) * SIDE] for b in range(nb)], 1)

    def unblock(wide):
        return jnp.concatenate([wide[:, b * cols:(b + 1) * cols] for b in range(nb)], 0)

    def stack(value):
        return jnp.concatenate(split(value), 0)

    def across(wide):
        high, low = split(wide)
        return jnp.concatenate([unblock(high), unblock(low)], 1)

    def of(gs):
        return [(n, PAIR * g + i) for n, g in enumerate(gs) for i in range(PAIR)]

    def x_mask(l):
        return blocks(wet[l])

    def y_mask(l):
        return wet_t[l]

    def firsts(gs, rhs, dim, weights, mask_of):
        closing, opening = [None] * len(gs), [None] * len(gs)
        masked = []
        for (n, l), side in zip(of(gs), rhs):
            both = dot(weights[l, pl.ds(0, 2 * SIDE + 16), :], side, 1, dim)
            held = both[:SIDE] + both[SIDE:2 * SIDE]
            inside[l] = held
            closing[n] = plus(closing[n], halves(both[2 * SIDE:]))
            masked.append(stack(held * mask_of(l)))
        for (n, l), side in zip(of(gs), masked):
            opening[n] = plus(opening[n], halves(dot(weights[l, pl.ds(2 * SIDE + 16, 16), :], side)))
        return [tiles(value) for value in closing], [tiles(value) for value in opening]

    def seconds(gs, starts, lasts, weights, answers, mask_of):
        ahead = [three(jnp.concatenate(tile, 1)) for tile in starts]
        behind = [three(jnp.concatenate(tile, 1)) for tile in lasts]
        sides = []
        for n, l in of(gs):
            field = (inside[l] + dot(answers[l], ahead[n])) * mask_of(l)
            high, low = split(field)
            sides.append(jnp.concatenate([high, low, high, behind[n]], 0))
        return [dot(weights[l], side) * mask_of(l) for (n, l), side in zip(of(gs), sides)]

    def halves(both):
        return both[:8] + both[8:16]

    def tiles(wide):
        return [wide[:, t * 128:(t + 1) * 128] for t in range(wide.shape[1] // 128)]

    def plus(total, piece):
        return piece if total is None else total + piece

    def packed(first, second, k):
        t, off = (k * share) // 128, (k * share) % 128
        return jnp.where(left, slide(first[t], -off), slide(second[t], mid - off))

    def x_first(gs, rhs, dim, rep):
        closings, openings = firsts(gs, rhs, dim, wx, x_mask)
        for g, closing, opening in zip(gs, closings, openings):
            carry = closing[0]
            chain = [opening[0]]
            ends_x[g, 0] = opening[0]
            for n in range(1, nb):
                turns = turned(carry)
                before[g, n - 1] = carry
                ends_x[g, n] = opening[n]
                chain.append(opening[n] + mixed([block_x[g, j, :, pl.ds(n * 128, 128)] for j in range(4)], turns))
                carry = advance(turns, coef_x, g, 0) + closing[n]
            end = chain[-1]
            for n in range(nb - 2, -1, -1):
                end = advance(turned(end), coef_x, g, 0) + chain[n]
            message = jnp.concatenate([carry, end], 0)
            end_x[rep, g] = message
            got_x[rep, g, gx] = message
        for g in gs:
            for d in range(1, nx):
                x_copy(g, rep, d).start()

    def x_entries(g, rep):
        carry = got_x[rep, g, 0, pl.ds(0, 8)]
        zero = jnp.zeros_like(carry)
        come = zero
        ending = [None] * nx
        for j in range(1, nx):
            turns = turned(carry)
            come = jnp.where(gx == j, carry, come)
            ending[j] = got_x[rep, g, j, pl.ds(8, 8)] + mixed(
                [mix_x[g, j, pl.ds(8 * k, 8)] for k in range(4)], turns
            )
            if j < nx - 1:
                carry = advance(turns, coef_x, g, nb - 1) + got_x[rep, g, j, pl.ds(0, 8)]
        carry = ending[nx - 1]
        leave = jnp.where(gx == nx - 2, carry, zero)
        for j in range(nx - 2, 0, -1):
            carry = advance(turned(carry), coef_x, g, nb - 1) + ending[j]
            leave = jnp.where(gx == j - 1, carry, leave)
        turns = turned(come)
        starts = [come] + [advance(turns, coef_x, g, n - 1) + before[g, n - 1] for n in range(1, nb)]
        lasts = [None] * nb
        lasts[nb - 1] = leave
        for n in range(nb - 1, 0, -1):
            ending_n = ends_x[g, n] + mixed(
                [block_x[g, j, :, pl.ds(n * 128, 128)] for j in range(4)], turned(starts[n])
            )
            lasts[n - 1] = advance(turned(lasts[n]), coef_x, g, 0) + ending_n
        return starts, lasts

    def x_second(gs, rep):
        for g in gs:
            @pl.when(rep == 0)
            def _():
                taken(mix_x.at[g, pl.ds(0, nx - 1)], rmx.at[g])

            taken(got_x.at[rep, g, pl.ds(0, nx - 1)], rx_sem.at[rep, g])
        starts, lasts = zip(*[x_entries(g, rep) for g in gs])
        return seconds(gs, starts, lasts, bx, rx, x_mask)

    def y_first(gs, fields, rep):
        closings, openings = firsts(gs, [across(field) for field in fields], 1, wy, y_mask)
        for g, closing, opening in zip(gs, closings, openings):
            for k in range(ny):
                end_y[rep, g, k] = packed(closing, opening, k)
            got_y[rep, g, gy] = end_y[rep, g, gy]
        for g in gs:
            for d in range(1, ny):
                y_copy(g, rep, d).start()

    def y_owner(gs, rep):
        for g in gs:
            @pl.when(rep == 0)
            def _():
                taken(got_m.at[g, pl.ds(0, ny - 1)], rmy.at[g])

            taken(got_y.at[rep, g, pl.ds(0, ny - 1)], ry_sem.at[rep, g])
        for g in gs:
            got = [got_y[rep, g, j] for j in range(ny)]
            first = [jnp.where(left, tile, slide(tile, mid)) for tile in got]
            starts, ending = [None] * ny, [None] * ny
            starts[0] = jnp.zeros_like(first[0])
            carry = first[0]
            for j in range(1, ny):
                turns = turned(carry)
                starts[j] = carry
                even, odd = got_m[g, j, pl.ds(0, 8)], got_m[g, j, pl.ds(8, 8)]
                ending[j] = got[j] + mixed([slide(even, mid), even, slide(odd, mid), odd], turns)
                if j < ny - 1:
                    carry = advance(turns, coef_y, g, 0) + first[j]
            last = jnp.zeros_like(carry)
            for j in range(ny - 1, -1, -1):
                back_y[rep, g, j] = jnp.where(left, starts[j], last)
                if j:
                    last = ending[j] if j == ny - 1 else advance(turned(last), coef_y, g, 0) + ending[j]
            come_y[rep, g, gy] = back_y[rep, g, gy]
        for g in gs:
            for d in range(1, ny):
                b_copy(g, rep, d).start()

    def y_entries(g, rep):
        starts, lasts = [None] * (rows // 128), [None] * (rows // 128)
        for k in range(ny):
            t, off = (k * share) // 128, (k * share) % 128
            tile = come_y[rep, g, k]
            start, last = slide(tile, off), slide(tile, off - mid)
            if off == 0:
                starts[t], lasts[t] = start, last
            else:
                starts[t] = jnp.where(lane >= off, start, starts[t])
                lasts[t] = jnp.where(lane >= off, last, lasts[t])
        return starts, lasts

    def y_second(gs, rep):
        for g in gs:
            taken(come_y.at[rep, g, pl.ds(0, ny - 1)], rb.at[rep, g])
        starts, lasts = zip(*[y_entries(g, rep) for g in gs])
        return seconds(gs, starts, lasts, by, ry, y_mask)

    def each(body, team=1):
        def step(s, c):
            body([team * s + n for n in range(team)])
            return c

        lax.fori_loop(0, groups // team, step, 0)

    sources = ((sea_hbm, sea), (inc_hbm, inc), (dev_hbm, dev))

    def incoming(l, n):
        src, dst = sources[n]
        return pltpu.make_async_copy(src.at[l], dst.at[l], in_sem.at[n, l])

    few = [
        pltpu.make_async_copy(src, dst, few_sem.at[n])
        for n, (src, dst) in enumerate(((steps_hbm, steps), (rate_x_hbm, rate_x), (rate_y_hbm, rate_y)))
    ]
    for copy in few:
        copy.start()
    for l in range(levels):
        for n in range(3):
            incoming(l, n).start()

    lags = (
        lax.broadcasted_iota(jnp.int32, (SIDE, SIDE), 0) - lax.broadcasted_iota(jnp.int32, (SIDE, SIDE), 1)
    ).astype(f32)

    def shape_of(lag):
        span = jnp.maximum(lag, 0.0)
        return span, jnp.where(lag > -0.5, (span + 1.0) * (span + 2.0) * (span + 3.0) / 6.0, 0.0)

    near = (shape_of(lags), shape_of(-lags))

    def tile(shape, rate, weight):
        weight4 = weight * weight * weight * weight
        weight4 = jnp.concatenate([weight4] * (SIDE // 8), 0)
        return split(weight4 * shape[1] * jnp.exp(-rate * shape[0]))

    def by_row(values, i):
        total = jnp.zeros(row.shape, f32)
        for k, value in enumerate(values):
            total = jnp.where(row == k + 4 * i, value, total)
        return total

    def powers(weight):
        return [jnp.ones_like(weight), weight, weight * weight, weight * weight * weight]

    def final_of(i, places, rate, weight):
        pw, leave = powers(weight), binomials(places + 1.0)
        return by_row([weight * pw[k] * leave[k] for k in range(4)], i) * jnp.exp(-rate * places)

    def answer_of(i, places, rate, weight):
        pw, ahead = powers(weight), places + 1.0
        come = binomials(ahead)
        return by_row([pw[3 - k] * come[3 - k] for k in range(4)], i) * jnp.exp(-rate * ahead)

    def high_low(value):
        high = value.astype(bf16).astype(f32)
        return high, value - high

    def finals(i, back, rate, weight):
        over = lane.astype(f32)
        high, low = high_low(final_of(i, over if back else SIDE - 1.0 - over, rate, weight))
        return jnp.concatenate([high, low], 0).astype(bf16)

    def answers(i, back, rate, weight):
        over = lane.astype(f32)
        high, low = high_low(answer_of(i, SIDE - 1.0 - over if back else over, rate, weight))
        return [high, high, low, jnp.zeros_like(high)]

    def filters(first, second, reply, g, rates, weights):
        zero = jnp.zeros((SIDE, SIDE), bf16)
        lower, upper = pl.ds(0, SIDE), pl.ds(SIDE, SIDE)
        replies = []
        for i in range(PAIR):
            l = PAIR * g + i
            rate, weight = rates[i], weights[i]
            high, low = tile(near[0], rate, weight)
            first[l, lower, lower] = high
            first[l, lower, upper] = high
            first[l, upper, lower] = low
            first[l, upper, upper] = zero
            high, low = tile(near[1], rate, weight)
            second[l, :, lower] = high
            second[l, :, upper] = high
            second[l, :, pl.ds(2 * SIDE, SIDE)] = low
            for back in (0, 1):
                final = finals(i, back, rate, weight)
                first[l, pl.ds(2 * SIDE + 16 * back, 16), lower] = final
                first[l, pl.ds(2 * SIDE + 16 * back, 16), upper] = final
                replies += answers(i, back, rate, weight)
        turn = jnp.concatenate(replies, 0).T
        for i in range(PAIR):
            l = PAIR * g + i
            for back in (0, 1):
                part = slide(turn, -32 * (2 * i + back))[:, :32].astype(bf16)
                if back:
                    second[l, :, pl.ds(3 * SIDE, 32)] = part
                else:
                    reply[l] = part

    def products(i, places, rate, weight):
        final = final_of(i, places, rate, weight)
        turns = turned(answer_of(i, places, rate, weight))
        parts = []
        for j in range(4):
            turn = turns[0] if j == 0 else jnp.where(place >= j, turns[j], pltpu.roll(turns[0], j + 4, 0))
            parts += list(high_low(final * turn))
        return jnp.concatenate(parts, 0).astype(bf16)

    def coefs(coef, g, spans, rates, weights):
        low = row < 4
        rate = jnp.where(low, rates[0], rates[1])
        weight = jnp.where(low, weights[0], weights[1])
        power = (jnp.ones_like(weight), weight, weight * weight, weight * weight * weight)
        for n, span in enumerate(spans):
            fall = jnp.exp(-rate * span)
            count = (1.0, span, span * (span + 1.0) / 2.0, span * (span + 1.0) * (span + 2.0) / 6.0)
            for j in range(4):
                coef[g, 4 * n + j] = jnp.where(place >= j, fall * (power[j] * count[j]), 0.0)

    def build_x(g):
        two = [PAIR * g + i for i in range(PAIR)]
        rates = [rate_x[l] for l in two]
        weights = [section_gain(rate_x[l], steps[l]) for l in two]
        filters(wx, bx, rx, g, rates, weights)
        for i, l in enumerate(two):
            for b in range(nb):
                places = lane.astype(f32) + float(b * SIDE)
                tx[l, :, pl.ds(b * SIDE, SIDE)] = products(i, places, rates[i], weights[i])
        spans = [float(SIDE * n) for n in range(1, nb)] + [float(rows)]
        coefs(coef_x, g, spans, rates, weights)

    def build_y(g):
        two = [PAIR * g + i for i in range(PAIR)]
        rates = [rate_y[l] for l in two]
        weights = [section_gain(rate_y[l], steps[l]) for l in two]
        filters(wy, by, ry, g, rates, weights)
        for i, l in enumerate(two):
            ty[l, pl.ds(0, SIDE)] = jnp.where(lags == 0.0, 1.0, 0.0).astype(bf16)
            ty[l, pl.ds(SIDE, 64)] = products(i, lane.astype(f32), rates[i], weights[i])
        coefs(coef_y, g, [float(cols)], rates, weights)

    barrier = pltpu.get_barrier_semaphore()
    for d in range(1, nx):
        pl.semaphore_signal(barrier, inc=1, device_id=x_peer(d), device_id_type=MESH)
    for d in range(1, ny):
        pl.semaphore_signal(barrier, inc=1, device_id=y_peer(d), device_id_type=MESH)

    for copy in few:
        copy.wait()
    each(lambda gs: build_x(gs[0]))
    pl.semaphore_wait(barrier, nx + ny - 2)

    def four(wide):
        return [halves(wide[16 * j:16 * j + 16]) for j in range(4)]

    def begin_x(gs):
        device, block = [None] * len(gs), [None] * len(gs)
        for n, l in of(gs):
            incoming(l, 0).wait()
        for n, l in of(gs):
            mask = sea[l].astype(f32)
            wet[l] = mask
            mask = mask.astype(bf16)
            device[n] = plus(device[n], dot(tx[l], mask))
            block[n] = plus(block[n], dot(tx[l, :, pl.ds(0, SIDE)], blocks(mask)))
        for n, g in enumerate(gs):
            mix_x[g, gx] = jnp.concatenate(four(device[n]), 0)
            for d in range(1, nx):
                mx_copy(g, d).start()
            for j, part in enumerate(four(block[n])):
                block_x[g, j] = part
        for n, l in of(gs):
            for m in (1, 2):
                incoming(l, m).wait()
        x_first(gs, [stack(blocks(dev[l] * wet[l] * inc[l])) for n, l in of(gs)], 0, 0)

    def begin_y(gs):
        for g in gs:
            build_y(g)
        mixes = [None] * len(gs)
        for n, l in of(gs):
            both = dot(ty[l], wet[l].astype(bf16), 1, 1)
            wet_t[l] = both[:SIDE]
            mixes[n] = plus(mixes[n], both[SIDE:])
        for n, g in enumerate(gs):
            parts = [tiles(part) for part in four(mixes[n])]
            for k in range(ny):
                mix_y[g, k] = jnp.concatenate([packed(parts[0], parts[1], k), packed(parts[2], parts[3], k)], 0)
            got_m[g, gy] = mix_y[g, gy]
            for d in range(1, ny):
                my_copy(g, d).start()

    each(begin_x, TEAM)
    each(begin_y, TEAM)

    def repetition(rep, c):
        each(lambda gs: y_first(gs, x_second(gs, rep), rep), TEAM)
        each(lambda gs: y_owner(gs, rep), TEAM)

        @pl.when(rep < MAXSTEPS - 1)
        def _():
            def more(gs):
                fields = y_second(gs, rep)
                for (n, l), field in zip(of(gs), fields):
                    kept[l] = field
                x_first(gs, [across(field) for field in fields], 1, rep + 1)

            each(more, TEAM)

        @pl.when(rep == MAXSTEPS - 1)
        def _():
            def last(gs):
                fields = y_second(gs, rep)
                for (n, l), field in zip(of(gs), fields):
                    field = jnp.where(steps[l] > rep, field, kept[l])
                    for b in range(nb):
                        own = pl.ds(b * SIDE, SIDE)
                        out[l, own] = dev[l, own] * field[:, b * SIDE:(b + 1) * SIDE].T

            each(last, TEAM)

        return c

    lax.fori_loop(0, MAXSTEPS, repetition, 0)

    for d in range(1, nx):
        taken(mix_x.at[:, 0], smx.at[d - 1])
        for rep in range(MAXSTEPS):
            taken(end_x.at[rep], sx.at[rep, d - 1])
    for d in range(1, ny):
        taken(mix_y.at[:, 0], smy.at[d - 1])
        for rep in range(MAXSTEPS):
            taken(end_y.at[rep, :, 0], sy.at[rep, d - 1])
            taken(back_y.at[rep, :, 0], sb.at[rep, d - 1])


def on_device(nx, ny, increment, deviation, land_sea, filter_steps, zonal_rate, meridional_rate):
    levels, rows, cols = increment.shape
    nb = rows // SIDE
    groups = levels // PAIR
    hbm = pl.BlockSpec(memory_space=pltpu.HBM)
    vmem = pl.BlockSpec(memory_space=pltpu.VMEM)
    reps = MAXSTEPS
    dma = pltpu.SemaphoreType.DMA
    return pl.pallas_call(
        functools.partial(kernel, nx, ny, levels, rows, cols),
        out_shape=jax.ShapeDtypeStruct(increment.shape, f32),
        in_specs=[hbm] * 6,
        out_specs=vmem,
        scratch_shapes=[
            pltpu.SMEM((levels,), jnp.int32),
            pltpu.SMEM((levels,), f32),
            pltpu.SMEM((levels,), f32),
            pltpu.VMEM((levels, 2 * SIDE + 32, 2 * SIDE), bf16),
            pltpu.VMEM((levels, SIDE, 3 * SIDE + 32), bf16),
            pltpu.VMEM((levels, SIDE, 32), bf16),
            pltpu.VMEM((levels, 2 * SIDE + 32, 2 * SIDE), bf16),
            pltpu.VMEM((levels, SIDE, 3 * SIDE + 32), bf16),
            pltpu.VMEM((levels, SIDE, 32), bf16),
            pltpu.VMEM((levels, 64, rows), bf16),
            pltpu.VMEM((levels, SIDE + 64, cols), bf16),
            pltpu.VMEM((groups, 4 * nb, 8, 128), f32),
            pltpu.VMEM((groups, 4, 8, 128), f32),
            pltpu.VMEM((levels, SIDE, nb * cols), f32),
            pltpu.VMEM((groups, nb - 1, 8, cols), f32),
            pltpu.VMEM((groups, nb, 8, cols), f32),
            pltpu.VMEM((groups, 4, 8, nb * cols), f32),
            pltpu.VMEM((groups, nx, 32, cols), f32),
            pltpu.VMEM((groups, ny, 16, 128), f32),
            pltpu.VMEM((groups, ny, 16, 128), f32),
            pltpu.VMEM((reps, groups, 16, cols), f32),
            pltpu.VMEM((reps, groups, nx, 16, cols), f32),
            pltpu.VMEM((reps, groups, ny, 8, 128), f32),
            pltpu.VMEM((reps, groups, ny, 8, 128), f32),
            pltpu.VMEM((reps, groups, ny, 8, 128), f32),
            pltpu.VMEM((reps, groups, ny, 8, 128), f32),
            pltpu.VMEM((levels, rows, cols), f32),
            pltpu.VMEM((levels, rows, cols), f32),
            pltpu.VMEM((levels, rows, cols), jnp.int32),
            pltpu.VMEM((levels, rows, cols), f32),
            pltpu.VMEM((levels, cols, rows), f32),
            pltpu.VMEM((levels, cols, rows), f32),
            dma((nx - 1,)),
            dma((groups,)),
            dma((ny - 1,)),
            dma((groups,)),
            dma((reps, nx - 1)),
            dma((reps, groups)),
            dma((reps, ny - 1)),
            dma((reps, groups)),
            dma((reps, ny - 1)),
            dma((reps, groups)),
            dma((3, levels)),
            dma((3,)),
        ],
        compiler_params=pltpu.CompilerParams(
            collective_id=0, has_side_effects=True, vmem_limit_bytes=40 * 1024 * 1024
        ),
    )(
        *(
            pltpu.with_memory_space_constraint(a, pltpu.HBM)
            for a in (filter_steps, zonal_rate, meridional_rate, increment, deviation, land_sea)
        )
    )


def solution(mesh):
    placed = (P(None, "gx", "gy"), P(None, "gx", "gy"), P(None, "gx", "gy"), P(), P(), P())
    body = functools.partial(on_device, mesh.shape["gx"], mesh.shape["gy"])
    return jax.shard_map(
        body, mesh=mesh, in_specs=placed, out_specs=P(None, "gx", "gy"), check_vma=False
    )
```

time: 48.6 us -> 42.3 us (0.87)
  Pallas kernels: 43.7 us -> 40.8 us
  local copies, waits for them, and re-layouts: 3.28 us -> 1.32 us
  other arithmetic: 1.37 us -> 0 us
    pallas_call x1, Pallas kernels: 43.7 us -> 40.8 us  [on_device(): pl.pallas_call(functools.partial(kernel, nx, ny, levels, rows, cols), out...]
    unnamed x7 -> x1, local copies, waits for them, and re-layouts: 3.28 us -> 1.32 us
    mul x1 -> x0, other arithmetic: 0.71 us -> none  [section_gain(): return gain_base * fading ** (1.0 - 1.0 / (16.0 * filter_steps.astype(f32)))]
    sub x1 -> x0, other arithmetic: 0.66 us -> none  [section_gain(): return gain_base * fading ** (1.0 - 1.0 / (16.0 * filter_steps.astype(f32)))]
where the time goes in v2:
time: 42.3 us; the launch traced here: 42.2 us
  Pallas kernels  40.8 us (96%)
  local copies, waits for them, and re-layouts  1.32 us (3%)
    pallas_call x1, Pallas kernels, on_device(): pl.pallas_call(functools.partial(kernel, nx, ny, levels, rows, cols), out...  40.8 us
    unnamed x1, local copies, waits for them, and re-layouts  1.32 us

profile of v2, /device:TPU:0, one launch (start us, length us, event | category | flops | bytes accessed | tf_op | source)
XLA Modules:
  0.0 42.2 jit_solution(1470441180262256092)
XLA Ops:
  0.0 40.8 %shard_map.64 = f32[8,512,128]{2,1,0:T(8,128)S(1)} custom-call(s32[8]{0:T(128)} %steps_hbm.1, f32[8]{0:T(128)} %rate_x_hbm.1, f32[8]{0:T(128)} %rate_y_hbm.1, f32[8,512,128]{2,1,0:T(8,128)} %inc_hbm.1, f32[8,512,128]{2,1,0:T(8,128)} %dev_hbm.1, s32[8,512,128]{2,1,0:T(8,128)} %sea_hbm.1), custom_call_target="tpu_custom_call" | custom-call | tf_op jit(solution)/shard_map/pallas_call | solution.py:561
  40.8 1.3 %copy.8 = f32[8,512,128]{2,1,0:T(8,128)} copy(f32[8,512,128]{2,1,0:T(8,128)S(1)} %shard_map.64) | data formatting | bytes 4194304

commit v3 on v2

--- a/solution.py
+++ b/solution.py
@@ -63,12 +63,14 @@
     gx, gy = lax.axis_index("gx"), lax.axis_index("gy")
     nb = rows // SIDE
     groups = levels // PAIR
-    share = rows // ny
-    mid = 64
+    owners = ny // 2
+    least = ny // 4
+    share = rows // owners
+    mine = jnp.clip(gy - least, 0, owners - 1)
+    is_owner = (gy >= least) & (gy < least + owners)
     row = lax.broadcasted_iota(jnp.int32, (8, 128), 0)
     lane = lax.broadcasted_iota(jnp.int32, (8, 128), 1)
     place = jnp.where(row < 4, row, row - 4)
-    left = lane < mid
 
     def turned(state):
         return [state] + [pltpu.roll(state, j, 0) for j in range(1, 4)]
@@ -103,11 +105,15 @@
             device_id=x_peer(d), device_id_type=MESH,
         )
 
-    def my_copy(g, d):
+    def to_owner(d):
+        k = lax.rem(gy + d, owners)
+        return k, least + k != gy
+
+    def my_copy(g, k, d):
         return pltpu.make_async_remote_copy(
-            src_ref=mix_y.at[g, lax.rem(gy + d, ny)], dst_ref=got_m.at[g, gy],
-            send_sem=smy.at[d - 1], recv_sem=rmy.at[g],
-            device_id=y_peer(d), device_id_type=MESH,
+            src_ref=mix_y.at[g, k], dst_ref=got_m.at[g, gy],
+            send_sem=smy.at[d], recv_sem=rmy.at[g],
+            device_id=(gx, least + k), device_id_type=MESH,
         )
 
     def x_copy(g, rep, d):
@@ -117,16 +123,16 @@
             device_id=x_peer(d), device_id_type=MESH,
         )
 
-    def y_copy(g, rep, d):
+    def y_copy(g, rep, k, d):
         return pltpu.make_async_remote_copy(
-            src_ref=end_y.at[rep, g, lax.rem(gy + d, ny)], dst_ref=got_y.at[rep, g, gy],
-            send_sem=sy.at[rep, d - 1], recv_sem=ry_sem.at[rep, g],
-            device_id=y_peer(d), device_id_type=MESH,
+            src_ref=end_y.at[rep, g, k], dst_ref=got_y.at[rep, g, gy],
+            send_sem=sy.at[rep, d], recv_sem=ry_sem.at[rep, g],
+            device_id=(gx, least + k), device_id_type=MESH,
         )
 
     def b_copy(g, rep, d):
         return pltpu.make_async_remote_copy(
-            src_ref=back_y.at[rep, g, lax.rem(gy + d, ny)], dst_ref=come_y.at[rep, g, gy],
+            src_ref=back_y.at[rep, g, lax.rem(gy + d, ny)], dst_ref=come_y.at[rep, g, mine],
             send_sem=sb.at[rep, d - 1], recv_sem=rb.at[rep, g],
             device_id=y_peer(d), device_id_type=MESH,
         )
@@ -188,9 +194,9 @@
     def plus(total, piece):
         return piece if total is None else total + piece
 
-    def packed(first, second, k):
+    def packed(parts, k):
         t, off = (k * share) // 128, (k * share) % 128
-        return jnp.where(left, slide(first[t], -off), slide(second[t], mid - off))
+        return jnp.concatenate([slide(part[t], -off) for part in parts], 0)
 
     def x_first(gs, rhs, dim, rep):
         closings, openings = firsts(gs, rhs, dim, wx, x_mask)
@@ -256,12 +262,16 @@
     def y_first(gs, fields, rep):
         closings, openings = firsts(gs, [across(field) for field in fields], 1, wy, y_mask)
         for g, closing, opening in zip(gs, closings, openings):
-            for k in range(ny):
-                end_y[rep, g, k] = packed(closing, opening, k)
-            got_y[rep, g, gy] = end_y[rep, g, gy]
-        for g in gs:
-            for d in range(1, ny):
-                y_copy(g, rep, d).start()
+            for k in range(owners):
+                end_y[rep, g, k] = packed([closing, opening], k)
+            got_y[rep, g, gy] = end_y[rep, g, mine]
+        for d in range(owners):
+            k, other = to_owner(d)
+
+            @pl.when(other)
+            def _():
+                for g in gs:
+                    y_copy(g, rep, k, d).start()
 
     def y_owner(gs, rep):
         for g in gs:
@@ -271,34 +281,33 @@
 
             taken(got_y.at[rep, g, pl.ds(0, ny - 1)], ry_sem.at[rep, g])
         for g in gs:
-            got = [got_y[rep, g, j] for j in range(ny)]
-            first = [jnp.where(left, tile, slide(tile, mid)) for tile in got]
             starts, ending = [None] * ny, [None] * ny
-            starts[0] = jnp.zeros_like(first[0])
-            carry = first[0]
+            carry = got_y[rep, g, 0, pl.ds(0, 8)]
+            starts[0] = jnp.zeros_like(carry)
             for j in range(1, ny):
                 turns = turned(carry)
                 starts[j] = carry
-                even, odd = got_m[g, j, pl.ds(0, 8)], got_m[g, j, pl.ds(8, 8)]
-                ending[j] = got[j] + mixed([slide(even, mid), even, slide(odd, mid), odd], turns)
+                ending[j] = got_y[rep, g, j, pl.ds(8, 8)] + mixed(
+                    [got_m[g, j, pl.ds(8 * m, 8)] for m in range(4)], turns
+                )
                 if j < ny - 1:
-                    carry = advance(turns, coef_y, g, 0) + first[j]
+                    carry = advance(turns, coef_y, g, 0) + got_y[rep, g, j, pl.ds(0, 8)]
             last = jnp.zeros_like(carry)
             for j in range(ny - 1, -1, -1):
-                back_y[rep, g, j] = jnp.where(left, starts[j], last)
+                back_y[rep, g, j] = jnp.concatenate([starts[j], last], 0)
                 if j:
                     last = ending[j] if j == ny - 1 else advance(turned(last), coef_y, g, 0) + ending[j]
-            come_y[rep, g, gy] = back_y[rep, g, gy]
+            come_y[rep, g, mine] = back_y[rep, g, gy]
         for g in gs:
             for d in range(1, ny):
                 b_copy(g, rep, d).start()
 
     def y_entries(g, rep):
         starts, lasts = [None] * (rows // 128), [None] * (rows // 128)
-        for k in range(ny):
+        for k in range(owners):
             t, off = (k * share) // 128, (k * share) % 128
-            tile = come_y[rep, g, k]
-            start, last = slide(tile, off), slide(tile, off - mid)
+            start = slide(come_y[rep, g, k, pl.ds(0, 8)], off)
+            last = slide(come_y[rep, g, k, pl.ds(8, 8)], off)
             if off == 0:
                 starts[t], lasts[t] = start, last
             else:
@@ -307,8 +316,12 @@
         return starts, lasts
 
     def y_second(gs, rep):
-        for g in gs:
-            taken(come_y.at[rep, g, pl.ds(0, ny - 1)], rb.at[rep, g])
+        for count, role in ((owners - 1, is_owner), (owners, jnp.logical_not(is_owner))):
+            @pl.when(role)
+            def _():
+                for g in gs:
+                    taken(come_y.at[rep, g, pl.ds(0, count)], rb.at[rep, g])
+
         starts, lasts = zip(*[y_entries(g, rep) for g in gs])
         return seconds(gs, starts, lasts, by, ry, y_mask)
 
@@ -464,7 +477,6 @@
     for copy in few:
         copy.wait()
     each(lambda gs: build_x(gs[0]))
-    pl.semaphore_wait(barrier, nx + ny - 2)
 
     def four(wide):
         return [halves(wide[16 * j:16 * j + 16]) for j in range(4)]
@@ -481,10 +493,16 @@
             block[n] = plus(block[n], dot(tx[l, :, pl.ds(0, SIDE)], blocks(mask)))
         for n, g in enumerate(gs):
             mix_x[g, gx] = jnp.concatenate(four(device[n]), 0)
+            for j, part in enumerate(four(block[n])):
+                block_x[g, j] = part
+
+        @pl.when(gs[0] == 0)
+        def _():
+            pl.semaphore_wait(barrier, nx + ny - 2)
+
+        for g in gs:
             for d in range(1, nx):
                 mx_copy(g, d).start()
-            for j, part in enumerate(four(block[n])):
-                block_x[g, j] = part
         for n, l in of(gs):
             for m in (1, 2):
                 incoming(l, m).wait()
@@ -500,18 +518,29 @@
             mixes[n] = plus(mixes[n], both[SIDE:])
         for n, g in enumerate(gs):
             parts = [tiles(part) for part in four(mixes[n])]
-            for k in range(ny):
-                mix_y[g, k] = jnp.concatenate([packed(parts[0], parts[1], k), packed(parts[2], parts[3], k)], 0)
-            got_m[g, gy] = mix_y[g, gy]
-            for d in range(1, ny):
-                my_copy(g, d).start()
-
-    each(begin_x, TEAM)
-    each(begin_y, TEAM)
+            for k in range(owners):
+                mix_y[g, k] = packed(parts, k)
+            got_m[g, gy] = mix_y[g, mine]
+        for d in range(owners):
+            k, other = to_owner(d)
+
+            @pl.when(other)
+            def _():
+                for g in gs:
+                    my_copy(g, k, d).start()
+
+    def begin(gs):
+        begin_x(gs)
+        begin_y(gs)
+
+    each(begin, TEAM)
 
     def repetition(rep, c):
         each(lambda gs: y_first(gs, x_second(gs, rep), rep), TEAM)
-        each(lambda gs: y_owner(gs, rep), TEAM)
+        @pl.when(is_owner)
+        def _():
+            each(lambda gs: y_owner(gs, rep), TEAM)
+
 
         @pl.when(rep < MAXSTEPS - 1)
         def _():
@@ -543,11 +572,20 @@
         taken(mix_x.at[:, 0], smx.at[d - 1])
         for rep in range(MAXSTEPS):
             taken(end_x.at[rep], sx.at[rep, d - 1])
-    for d in range(1, ny):
-        taken(mix_y.at[:, 0], smy.at[d - 1])
-        for rep in range(MAXSTEPS):
-            taken(end_y.at[rep, :, 0], sy.at[rep, d - 1])
-            taken(back_y.at[rep, :, 0], sb.at[rep, d - 1])
+    for d in range(owners):
+        k, other = to_owner(d)
+
+        @pl.when(other)
+        def _():
+            taken(mix_y.at[:, 0], smy.at[d])
+            for rep in range(MAXSTEPS):
+                taken(end_y.at[rep, :, 0], sy.at[rep, d])
+
+    @pl.when(is_owner)
+    def _():
+        for d in range(1, ny):
+            for rep in range(MAXSTEPS):
+                taken(back_y.at[rep, :, 0], sb.at[rep, d - 1])
 
 
 def on_device(nx, ny, increment, deviation, land_sea, filter_steps, zonal_rate, meridional_rate):
@@ -582,14 +620,14 @@
             pltpu.VMEM((groups, nb, 8, cols), f32),
             pltpu.VMEM((groups, 4, 8, nb * cols), f32),
             pltpu.VMEM((groups, nx, 32, cols), f32),
-            pltpu.VMEM((groups, ny, 16, 128), f32),
-            pltpu.VMEM((groups, ny, 16, 128), f32),
+            pltpu.VMEM((groups, ny // 2, 32, 128), f32),
+            pltpu.VMEM((groups, ny, 32, 128), f32),
             pltpu.VMEM((reps, groups, 16, cols), f32),
             pltpu.VMEM((reps, groups, nx, 16, cols), f32),
-            pltpu.VMEM((reps, groups, ny, 8, 128), f32),
-            pltpu.VMEM((reps, groups, ny, 8, 128), f32),
-            pltpu.VMEM((reps, groups, ny, 8, 128), f32),
-            pltpu.VMEM((reps, groups, ny, 8, 128), f32),
+            pltpu.VMEM((reps, groups, ny // 2, 16, 128), f32),
+            pltpu.VMEM((reps, groups, ny, 16, 128), f32),
+            pltpu.VMEM((reps, groups, ny, 16, 128), f32),
+            pltpu.VMEM((reps, groups, ny // 2, 16, 128), f32),
             pltpu.VMEM((levels, rows, cols), f32),
             pltpu.VMEM((levels, rows, cols), f32),
             pltpu.VMEM((levels, rows, cols), jnp.int32),
@@ -598,11 +636,11 @@
             pltpu.VMEM((levels, cols, rows), f32),
             dma((nx - 1,)),
             dma((groups,)),
-            dma((ny - 1,)),
+            dma((ny // 2,)),
             dma((groups,)),
             dma((reps, nx - 1)),
             dma((reps, groups)),
-            dma((reps, ny - 1)),
+            dma((reps, ny // 2)),
             dma((reps, groups)),
             dma((reps, ny - 1)),
             dma((reps, groups)),

time: 42.3 us -> 40.3 us (0.953)
  Pallas kernels: 40.8 us -> 38.9 us
    pallas_call x1, Pallas kernels: 40.8 us -> 38.9 us  [on_device(): pl.pallas_call(functools.partial(kernel, nx, ny, levels, rows, cols), out...]
where the time goes in v3:
time: 40.3 us; the launch traced here: 40.2 us
  Pallas kernels  38.9 us (97%)
  local copies, waits for them, and re-layouts  1.32 us (3%)
    pallas_call x1, Pallas kernels, on_device(): pl.pallas_call(functools.partial(kernel, nx, ny, levels, rows, cols), out...  38.9 us
    unnamed x1, local copies, waits for them, and re-layouts  1.32 us

profile of v3, /device:TPU:0, one launch (start us, length us, event | category | flops | bytes accessed | tf_op | source)
XLA Modules:
  0.0 40.2 jit_solution(16056377107770928998)
XLA Ops:
  0.0 38.9 %shard_map.64 = f32[8,512,128]{2,1,0:T(8,128)S(1)} custom-call(s32[8]{0:T(128)} %steps_hbm.1, f32[8]{0:T(128)} %rate_x_hbm.1, f32[8]{0:T(128)} %rate_y_hbm.1, f32[8,512,128]{2,1,0:T(8,128)} %inc_hbm.1, f32[8,512,128]{2,1,0:T(8,128)} %dev_hbm.1, s32[8,512,128]{2,1,0:T(8,128)} %sea_hbm.1), custom_call_target="tpu_custom_call" | custom-call | tf_op jit(solution)/shard_map/pallas_call | solution.py:599
  38.9 1.3 %copy.8 = f32[8,512,128]{2,1,0:T(8,128)} copy(f32[8,512,128]{2,1,0:T(8,128)S(1)} %shard_map.64) | data formatting | bytes 4194304

commit v4 on v3

--- a/solution.py
+++ b/solution.py
@@ -10,6 +10,7 @@
 SIDE = 128
 PAIR = 2
 TEAM = 2
+UNIQUE = 20
 MAXSTEPS = 2
 gain_base = 3.0**0.125
 MESH = pl.DeviceIdType.MESH
@@ -56,7 +57,7 @@
     out,
     steps, rate_x, rate_y,
     wx, bx, rx, wy, by, ry, tx, ty, coef_x, coef_y,
-    inside, before, ends_x, block_x, mix_x, mix_y, got_m,
+    inside, before, ends_x, block_x, mix_x, mix_y, got_m, full_y,
     end_x, got_x, end_y, got_y, back_y, come_y, inc, dev, sea, wet, wet_t, kept,
     smx, rmx, smy, rmy, sx, rx_sem, sy, ry_sem, sb, rb, in_sem, few_sem,
 ):
@@ -111,7 +112,7 @@
 
     def my_copy(g, k, d):
         return pltpu.make_async_remote_copy(
-            src_ref=mix_y.at[g, k], dst_ref=got_m.at[g, gy],
+            src_ref=mix_y.at[g, k, pl.ds(0, UNIQUE)], dst_ref=got_m.at[g, gy, pl.ds(0, UNIQUE)],
             send_sem=smy.at[d], recv_sem=rmy.at[g],
             device_id=(gx, least + k), device_id_type=MESH,
         )
@@ -193,6 +194,21 @@
 
     def plus(total, piece):
         return piece if total is None else total + piece
+
+    def folded(mix):
+        def one(m0, m1, m2, m3):
+            both = jnp.where(place < 2, m0, jnp.where(place == 2, pltpu.roll(m2, 2, 0), pltpu.roll(m2, 1, 0)))
+            return both, jnp.where(place < 3, m1, m3), jnp.where(row < 2, m3, pltpu.roll(m3, 6, 0))
+
+        found = [one(*each_tile) for each_tile in zip(*[tiles(part) for part in mix])]
+        return [jnp.concatenate(part, 1) for part in zip(*found)]
+
+    def unfolded(t0, t1, t2):
+        m0 = jnp.where(place == 2, pltpu.roll(t0, 1, 0), jnp.where(place == 3, pltpu.roll(t0, 3, 0), t0))
+        m1 = jnp.where(place == 3, pltpu.roll(t1, 2, 0), t1)
+        m2 = jnp.where(place == 0, pltpu.roll(t0, 6, 0), jnp.where(place < 3, pltpu.roll(t0, 7, 0), t0))
+        m3 = jnp.where(row < 2, t2, jnp.where(row < 6, pltpu.roll(t2, 2, 0), pltpu.roll(t2, 4, 0)))
+        return [m0, m1, m2, jnp.where(place == 3, t1, m3)]
 
     def packed(parts, k):
         t, off = (k * share) // 128, (k * share) % 128
@@ -277,8 +293,12 @@
         for g in gs:
             @pl.when(rep == 0)
             def _():
-                taken(got_m.at[g, pl.ds(0, ny - 1)], rmy.at[g])
-
+                taken(got_m.at[g, pl.ds(0, ny - 1), pl.ds(0, UNIQUE)], rmy.at[g])
+                for j in range(1, ny):
+                    parts = unfolded(*[got_m[g, j, pl.ds(8 * m, 8)] for m in range(3)])
+                    full_y[g, j] = jnp.concatenate(parts, 0)
+
+        for g in gs:
             taken(got_y.at[rep, g, pl.ds(0, ny - 1)], ry_sem.at[rep, g])
         for g in gs:
             starts, ending = [None] * ny, [None] * ny
@@ -288,7 +308,7 @@
                 turns = turned(carry)
                 starts[j] = carry
                 ending[j] = got_y[rep, g, j, pl.ds(8, 8)] + mixed(
-                    [got_m[g, j, pl.ds(8 * m, 8)] for m in range(4)], turns
+                    [full_y[g, j, pl.ds(8 * m, 8)] for m in range(4)], turns
                 )
                 if j < ny - 1:
                     carry = advance(turns, coef_y, g, 0) + got_y[rep, g, j, pl.ds(0, 8)]
@@ -517,7 +537,7 @@
             wet_t[l] = both[:SIDE]
             mixes[n] = plus(mixes[n], both[SIDE:])
         for n, g in enumerate(gs):
-            parts = [tiles(part) for part in four(mixes[n])]
+            parts = [tiles(part) for part in folded(four(mixes[n]))]
             for k in range(owners):
                 mix_y[g, k] = packed(parts, k)
             got_m[g, gy] = mix_y[g, mine]
@@ -577,7 +597,7 @@
 
         @pl.when(other)
         def _():
-            taken(mix_y.at[:, 0], smy.at[d])
+            taken(mix_y.at[:, 0, pl.ds(0, UNIQUE)], smy.at[d])
             for rep in range(MAXSTEPS):
                 taken(end_y.at[rep, :, 0], sy.at[rep, d])
 
@@ -620,7 +640,8 @@
             pltpu.VMEM((groups, nb, 8, cols), f32),
             pltpu.VMEM((groups, 4, 8, nb * cols), f32),
             pltpu.VMEM((groups, nx, 32, cols), f32),
-            pltpu.VMEM((groups, ny // 2, 32, 128), f32),
+            pltpu.VMEM((groups, ny // 2, 24, 128), f32),
+            pltpu.VMEM((groups, ny, 24, 128), f32),
             pltpu.VMEM((groups, ny, 32, 128), f32),
             pltpu.VMEM((reps, groups, 16, cols), f32),
             pltpu.VMEM((reps, groups, nx, 16, cols), f32),

time: 40.3 us -> 38.4 us (0.953)
  Pallas kernels: 38.9 us -> 36.9 us
    pallas_call x1, Pallas kernels: 38.9 us -> 36.9 us  [on_device(): pl.pallas_call(functools.partial(kernel, nx, ny, levels, rows, cols), out...]
where the time goes in v4:
time: 38.4 us; the launch traced here: 38.3 us
  Pallas kernels  36.9 us (96%)
  local copies, waits for them, and re-layouts  1.32 us (3%)
    pallas_call x1, Pallas kernels, on_device(): pl.pallas_call(functools.partial(kernel, nx, ny, levels, rows, cols), out...  36.9 us
    unnamed x1, local copies, waits for them, and re-layouts  1.32 us

profile of v4, /device:TPU:0, one launch (start us, length us, event | category | flops | bytes accessed | tf_op | source)
XLA Modules:
  0.0 38.3 jit_solution(4286207948760161230)
XLA Ops:
  0.0 36.9 %shard_map.64 = f32[8,512,128]{2,1,0:T(8,128)S(1)} custom-call(s32[8]{0:T(128)} %steps_hbm.1, f32[8]{0:T(128)} %rate_x_hbm.1, f32[8]{0:T(128)} %rate_y_hbm.1, f32[8,512,128]{2,1,0:T(8,128)} %inc_hbm.1, f32[8,512,128]{2,1,0:T(8,128)} %dev_hbm.1, s32[8,512,128]{2,1,0:T(8,128)} %sea_hbm.1), custom_call_target="tpu_custom_call" | custom-call | tf_op jit(solution)/shard_map/pallas_call | solution.py:619
  36.9 1.3 %copy.8 = f32[8,512,128]{2,1,0:T(8,128)} copy(f32[8,512,128]{2,1,0:T(8,128)S(1)} %shard_map.64) | data formatting | bytes 4194304

commit v5 on v4

--- a/solution.py
+++ b/solution.py
@@ -107,7 +107,7 @@
         )
 
     def to_owner(d):
-        k = lax.rem(gy + d, owners)
+        k = jnp.where(gy < ny // 2, owners - 1 - d, d)
         return k, least + k != gy
 
     def my_copy(g, k, d):
@@ -132,10 +132,13 @@
         )
 
     def b_copy(g, rep, d):
+        far = ny - d - (d >= ny - gy).astype(jnp.int32)
+        near = d - 1 + (d > gy).astype(jnp.int32)
+        target = jnp.where(gy < ny // 2, far, near)
         return pltpu.make_async_remote_copy(
-            src_ref=back_y.at[rep, g, lax.rem(gy + d, ny)], dst_ref=come_y.at[rep, g, mine],
+            src_ref=back_y.at[rep, g, target], dst_ref=come_y.at[rep, g, mine],
             send_sem=sb.at[rep, d - 1], recv_sem=rb.at[rep, g],
-            device_id=y_peer(d), device_id_type=MESH,
+            device_id=(gx, target), device_id_type=MESH,
         )
 
     def taken(ref, sem):
@@ -496,7 +499,7 @@
 
     for copy in few:
         copy.wait()
-    each(lambda gs: build_x(gs[0]))
+    each(lambda gs: [build_x(g) for g in gs], 2)
 
     def four(wide):
         return [halves(wide[16 * j:16 * j + 16]) for j in range(4)]
@@ -553,13 +556,13 @@
         begin_x(gs)
         begin_y(gs)
 
-    each(begin, TEAM)
+    each(begin, 2)
 
     def repetition(rep, c):
-        each(lambda gs: y_first(gs, x_second(gs, rep), rep), TEAM)
+        each(lambda gs: y_first(gs, x_second(gs, rep), rep), 1)
         @pl.when(is_owner)
         def _():
-            each(lambda gs: y_owner(gs, rep), TEAM)
+            each(lambda gs: y_owner(gs, rep), 1)
 
 
         @pl.when(rep < MAXSTEPS - 1)
@@ -570,7 +573,7 @@
                     kept[l] = field
                 x_first(gs, [across(field) for field in fields], 1, rep + 1)
 
-            each(more, TEAM)
+            each(more, 1)
 
         @pl.when(rep == MAXSTEPS - 1)
         def _():
@@ -582,7 +585,7 @@
                         own = pl.ds(b * SIDE, SIDE)
                         out[l, own] = dev[l, own] * field[:, b * SIDE:(b + 1) * SIDE].T
 
-            each(last, TEAM)
+            each(last, 1)
 
         return c
 

time: 38.4 us -> 35.6 us (0.927)
  Pallas kernels: 36.9 us -> 34.1 us
    pallas_call x1, Pallas kernels: 36.9 us -> 34.1 us  [on_device(): pl.pallas_call(functools.partial(kernel, nx, ny, levels, rows, cols), out...]
where the time goes in v5:
time: 35.6 us; the launch traced here: 35.5 us
  Pallas kernels  34.1 us (96%)
  local copies, waits for them, and re-layouts  1.32 us (4%)
    pallas_call x1, Pallas kernels, on_device(): pl.pallas_call(functools.partial(kernel, nx, ny, levels, rows, cols), out...  34.1 us
    unnamed x1, local copies, waits for them, and re-layouts  1.32 us

profile of v5, /device:TPU:0, one launch (start us, length us, event | category | flops | bytes accessed | tf_op | source)
XLA Modules:
  0.0 35.5 jit_solution(3460393657926215835)
XLA Ops:
  0.0 34.1 %shard_map.64 = f32[8,512,128]{2,1,0:T(8,128)S(1)} custom-call(s32[8]{0:T(128)} %steps_hbm.1, f32[8]{0:T(128)} %rate_x_hbm.1, f32[8]{0:T(128)} %rate_y_hbm.1, f32[8,512,128]{2,1,0:T(8,128)} %inc_hbm.1, f32[8,512,128]{2,1,0:T(8,128)} %dev_hbm.1, s32[8,512,128]{2,1,0:T(8,128)} %sea_hbm.1), custom_call_target="tpu_custom_call" | custom-call | tf_op jit(solution)/shard_map/pallas_call | solution.py:622
  34.1 1.3 %copy.8 = f32[8,512,128]{2,1,0:T(8,128)} copy(f32[8,512,128]{2,1,0:T(8,128)S(1)} %shard_map.64) | data formatting | bytes 4194304

commit v6 on v5

--- a/solution.py
+++ b/solution.py
@@ -169,8 +169,8 @@
     def firsts(gs, rhs, dim, weights, mask_of):
         closing, opening = [None] * len(gs), [None] * len(gs)
         masked = []
-        for (n, l), side in zip(of(gs), rhs):
-            both = dot(weights[l, pl.ds(0, 2 * SIDE + 16), :], side, 1, dim)
+        wides = [dot(weights[l, pl.ds(0, 2 * SIDE + 16), :], side, 1, dim) for (n, l), side in zip(of(gs), rhs)]
+        for (n, l), both in zip(of(gs), wides):
             held = both[:SIDE] + both[SIDE:2 * SIDE]
             inside[l] = held
             closing[n] = plus(closing[n], halves(both[2 * SIDE:]))
@@ -357,9 +357,10 @@
 
     sources = ((sea_hbm, sea), (inc_hbm, inc), (dev_hbm, dev))
 
-    def incoming(l, n):
+    def incoming(s, n):
         src, dst = sources[n]
-        return pltpu.make_async_copy(src.at[l], dst.at[l], in_sem.at[n, l])
+        own = pl.ds(s * PAIR * TEAM, PAIR * TEAM)
+        return pltpu.make_async_copy(src.at[own], dst.at[own], in_sem.at[n, s])
 
     few = [
         pltpu.make_async_copy(src, dst, few_sem.at[n])
@@ -367,9 +368,9 @@
     ]
     for copy in few:
         copy.start()
-    for l in range(levels):
+    for s in range(groups // TEAM):
         for n in range(3):
-            incoming(l, n).start()
+            incoming(s, n).start()
 
     lags = (
         lax.broadcasted_iota(jnp.int32, (SIDE, SIDE), 0) - lax.broadcasted_iota(jnp.int32, (SIDE, SIDE), 1)
@@ -418,27 +419,31 @@
         high, low = high_low(answer_of(i, SIDE - 1.0 - over if back else over, rate, weight))
         return [high, high, low, jnp.zeros_like(high)]
 
-    def filters(first, second, reply, g, rates, weights):
+    def filters_first(first, g, rates, weights):
         zero = jnp.zeros((SIDE, SIDE), bf16)
         lower, upper = pl.ds(0, SIDE), pl.ds(SIDE, SIDE)
-        replies = []
         for i in range(PAIR):
             l = PAIR * g + i
-            rate, weight = rates[i], weights[i]
-            high, low = tile(near[0], rate, weight)
+            high, low = tile(near[0], rates[i], weights[i])
             first[l, lower, lower] = high
             first[l, lower, upper] = high
             first[l, upper, lower] = low
             first[l, upper, upper] = zero
-            high, low = tile(near[1], rate, weight)
-            second[l, :, lower] = high
-            second[l, :, upper] = high
+            for back in (0, 1):
+                final = finals(i, back, rates[i], weights[i])
+                first[l, pl.ds(2 * SIDE + 16 * back, 16), lower] = final
+                first[l, pl.ds(2 * SIDE + 16 * back, 16), upper] = final
+
+    def filters_second(second, reply, g, rates, weights):
+        replies = []
+        for i in range(PAIR):
+            l = PAIR * g + i
+            high, low = tile(near[1], rates[i], weights[i])
+            second[l, :, pl.ds(0, SIDE)] = high
+            second[l, :, pl.ds(SIDE, SIDE)] = high
             second[l, :, pl.ds(2 * SIDE, SIDE)] = low
             for back in (0, 1):
-                final = finals(i, back, rate, weight)
-                first[l, pl.ds(2 * SIDE + 16 * back, 16), lower] = final
-                first[l, pl.ds(2 * SIDE + 16 * back, 16), upper] = final
-                replies += answers(i, back, rate, weight)
+                replies += answers(i, back, rates[i], weights[i])
         turn = jnp.concatenate(replies, 0).T
         for i in range(PAIR):
             l = PAIR * g + i
@@ -473,7 +478,8 @@
         two = [PAIR * g + i for i in range(PAIR)]
         rates = [rate_x[l] for l in two]
         weights = [section_gain(rate_x[l], steps[l]) for l in two]
-        filters(wx, bx, rx, g, rates, weights)
+        filters_first(wx, g, rates, weights)
+        filters_second(bx, rx, g, rates, weights)
         for i, l in enumerate(two):
             for b in range(nb):
                 places = lane.astype(f32) + float(b * SIDE)
@@ -485,11 +491,16 @@
         two = [PAIR * g + i for i in range(PAIR)]
         rates = [rate_y[l] for l in two]
         weights = [section_gain(rate_y[l], steps[l]) for l in two]
-        filters(wy, by, ry, g, rates, weights)
+        filters_first(wy, g, rates, weights)
         for i, l in enumerate(two):
             ty[l, pl.ds(0, SIDE)] = jnp.where(lags == 0.0, 1.0, 0.0).astype(bf16)
             ty[l, pl.ds(SIDE, 64)] = products(i, lane.astype(f32), rates[i], weights[i])
         coefs(coef_y, g, [float(cols)], rates, weights)
+
+    def build_later(g):
+        two = [PAIR * g + i for i in range(PAIR)]
+        weights = [section_gain(rate_y[l], steps[l]) for l in two]
+        filters_second(by, ry, g, [rate_y[l] for l in two], weights)
 
     barrier = pltpu.get_barrier_semaphore()
     for d in range(1, nx):
@@ -506,8 +517,7 @@
 
     def begin_x(gs):
         device, block = [None] * len(gs), [None] * len(gs)
-        for n, l in of(gs):
-            incoming(l, 0).wait()
+        incoming(gs[0] // TEAM, 0).wait()
         for n, l in of(gs):
             mask = sea[l].astype(f32)
             wet[l] = mask
@@ -526,9 +536,8 @@
         for g in gs:
             for d in range(1, nx):
                 mx_copy(g, d).start()
-        for n, l in of(gs):
-            for m in (1, 2):
-                incoming(l, m).wait()
+        for m in (1, 2):
+            incoming(gs[0] // TEAM, m).wait()
         x_first(gs, [stack(blocks(dev[l] * wet[l] * inc[l])) for n, l in of(gs)], 0, 0)
 
     def begin_y(gs):
@@ -556,10 +565,14 @@
         begin_x(gs)
         begin_y(gs)
 
-    each(begin, 2)
+    each(begin, TEAM)
 
     def repetition(rep, c):
         each(lambda gs: y_first(gs, x_second(gs, rep), rep), 1)
+        @pl.when(rep == 0)
+        def _():
+            each(lambda gs: [build_later(g) for g in gs], TEAM)
+
         @pl.when(is_owner)
         def _():
             each(lambda gs: y_owner(gs, rep), 1)
@@ -668,7 +681,7 @@
             dma((reps, groups)),
             dma((reps, ny - 1)),
             dma((reps, groups)),
-            dma((3, levels)),
+            dma((3, groups // TEAM)),
             dma((3,)),
         ],
         compiler_params=pltpu.CompilerParams(

time: 35.6 us -> 35.7 us (level)
  no operation moved by 1% of the time
where the time goes in v6:
time: 35.7 us; the launch traced here: 35.5 us
  Pallas kernels  34.2 us (96%)
  local copies, waits for them, and re-layouts  1.32 us (4%)
    pallas_call x1, Pallas kernels, on_device(): pl.pallas_call(functools.partial(kernel, nx, ny, levels, rows, cols), out...  34.2 us
    unnamed x1, local copies, waits for them, and re-layouts  1.32 us

profile of v6, /device:TPU:0, one launch (start us, length us, event | category | flops | bytes accessed | tf_op | source)
XLA Modules:
  0.0 35.5 jit_solution(9726674800865841042)
XLA Ops:
  0.0 34.2 %shard_map.64 = f32[8,512,128]{2,1,0:T(8,128)S(1)} custom-call(s32[8]{0:T(128)} %steps_hbm.1, f32[8]{0:T(128)} %rate_x_hbm.1, f32[8]{0:T(128)} %rate_y_hbm.1, f32[8,512,128]{2,1,0:T(8,128)} %inc_hbm.1, f32[8,512,128]{2,1,0:T(8,128)} %dev_hbm.1, s32[8,512,128]{2,1,0:T(8,128)} %sea_hbm.1), custom_call_target="tpu_custom_call" | custom-call | tf_op jit(solution)/shard_map/pallas_call | solution.py:635
  34.2 1.3 %copy.8 = f32[8,512,128]{2,1,0:T(8,128)} copy(f32[8,512,128]{2,1,0:T(8,128)S(1)} %shard_map.64) | data formatting | bytes 4194304

commit v7 on v5

--- a/solution.py
+++ b/solution.py
@@ -169,8 +169,8 @@
     def firsts(gs, rhs, dim, weights, mask_of):
         closing, opening = [None] * len(gs), [None] * len(gs)
         masked = []
-        for (n, l), side in zip(of(gs), rhs):
-            both = dot(weights[l, pl.ds(0, 2 * SIDE + 16), :], side, 1, dim)
+        wides = [dot(weights[l, pl.ds(0, 2 * SIDE + 16), :], side, 1, dim) for (n, l), side in zip(of(gs), rhs)]
+        for (n, l), both in zip(of(gs), wides):
             held = both[:SIDE] + both[SIDE:2 * SIDE]
             inside[l] = held
             closing[n] = plus(closing[n], halves(both[2 * SIDE:]))
@@ -357,9 +357,10 @@
 
     sources = ((sea_hbm, sea), (inc_hbm, inc), (dev_hbm, dev))
 
-    def incoming(l, n):
+    def incoming(s, n):
         src, dst = sources[n]
-        return pltpu.make_async_copy(src.at[l], dst.at[l], in_sem.at[n, l])
+        own = pl.ds(s * PAIR * TEAM, PAIR * TEAM)
+        return pltpu.make_async_copy(src.at[own], dst.at[own], in_sem.at[n, s])
 
     few = [
         pltpu.make_async_copy(src, dst, few_sem.at[n])
@@ -367,9 +368,9 @@
     ]
     for copy in few:
         copy.start()
-    for l in range(levels):
+    for s in range(groups // TEAM):
         for n in range(3):
-            incoming(l, n).start()
+            incoming(s, n).start()
 
     lags = (
         lax.broadcasted_iota(jnp.int32, (SIDE, SIDE), 0) - lax.broadcasted_iota(jnp.int32, (SIDE, SIDE), 1)
@@ -506,8 +507,7 @@
 
     def begin_x(gs):
         device, block = [None] * len(gs), [None] * len(gs)
-        for n, l in of(gs):
-            incoming(l, 0).wait()
+        incoming(gs[0] // TEAM, 0).wait()
         for n, l in of(gs):
             mask = sea[l].astype(f32)
             wet[l] = mask
@@ -526,9 +526,8 @@
         for g in gs:
             for d in range(1, nx):
                 mx_copy(g, d).start()
-        for n, l in of(gs):
-            for m in (1, 2):
-                incoming(l, m).wait()
+        for m in (1, 2):
+            incoming(gs[0] // TEAM, m).wait()
         x_first(gs, [stack(blocks(dev[l] * wet[l] * inc[l])) for n, l in of(gs)], 0, 0)
 
     def begin_y(gs):
@@ -556,7 +555,7 @@
         begin_x(gs)
         begin_y(gs)
 
-    each(begin, 2)
+    each(begin, TEAM)
 
     def repetition(rep, c):
         each(lambda gs: y_first(gs, x_second(gs, rep), rep), 1)
@@ -668,7 +667,7 @@
             dma((reps, groups)),
             dma((reps, ny - 1)),
             dma((reps, groups)),
-            dma((3, levels)),
+            dma((3, groups // TEAM)),
             dma((3,)),
         ],
         compiler_params=pltpu.CompilerParams(

time: 35.6 us -> 35.4 us (level)
  no operation moved by 1% of the time
where the time goes in v7:
time: 35.4 us; the launch traced here: 35.3 us
  Pallas kernels  34 us (96%)
  local copies, waits for them, and re-layouts  1.32 us (4%)
    pallas_call x1, Pallas kernels, on_device(): pl.pallas_call(functools.partial(kernel, nx, ny, levels, rows, cols), out...  34 us
    unnamed x1, local copies, waits for them, and re-layouts  1.32 us

profile of v7, /device:TPU:0, one launch (start us, length us, event | category | flops | bytes accessed | tf_op | source)
XLA Modules:
  0.0 35.3 jit_solution(9191840610424319865)
XLA Ops:
  0.0 34.0 %shard_map.64 = f32[8,512,128]{2,1,0:T(8,128)S(1)} custom-call(s32[8]{0:T(128)} %steps_hbm.1, f32[8]{0:T(128)} %rate_x_hbm.1, f32[8]{0:T(128)} %rate_y_hbm.1, f32[8,512,128]{2,1,0:T(8,128)} %inc_hbm.1, f32[8,512,128]{2,1,0:T(8,128)} %dev_hbm.1, s32[8,512,128]{2,1,0:T(8,128)} %sea_hbm.1), custom_call_target="tpu_custom_call" | custom-call | tf_op jit(solution)/shard_map/pallas_call | solution.py:621
  34.0 1.3 %copy.8 = f32[8,512,128]{2,1,0:T(8,128)} copy(f32[8,512,128]{2,1,0:T(8,128)S(1)} %shard_map.64) | data formatting | bytes 4194304

commit v8 on v7

--- a/solution.py
+++ b/solution.py
@@ -296,7 +296,7 @@
         for g in gs:
             @pl.when(rep == 0)
             def _():
-                taken(got_m.at[g, pl.ds(0, ny - 1), pl.ds(0, UNIQUE)], rmy.at[g])
+                taken(got_m.at[g, pl.ds(0, ny - 2), pl.ds(0, UNIQUE)], rmy.at[g])
                 for j in range(1, ny):
                     parts = unfolded(*[got_m[g, j, pl.ds(8 * m, 8)] for m in range(3)])
                     full_y[g, j] = jnp.concatenate(parts, 0)
@@ -546,7 +546,7 @@
         for d in range(owners):
             k, other = to_owner(d)
 
-            @pl.when(other)
+            @pl.when(other & (gy > 0))
             def _():
                 for g in gs:
                     my_copy(g, k, d).start()
@@ -599,7 +599,10 @@
 
         @pl.when(other)
         def _():
-            taken(mix_y.at[:, 0, pl.ds(0, UNIQUE)], smy.at[d])
+            @pl.when(gy > 0)
+            def _():
+                taken(mix_y.at[:, 0, pl.ds(0, UNIQUE)], smy.at[d])
+
             for rep in range(MAXSTEPS):
                 taken(end_y.at[rep, :, 0], sy.at[rep, d])
 

time: 35.4 us -> 35.5 us (level)
  no operation moved by 1% of the time
where the time goes in v8:
time: 35.5 us; the launch traced here: 35.4 us
  Pallas kernels  34.1 us (96%)
  local copies, waits for them, and re-layouts  1.32 us (4%)
    pallas_call x1, Pallas kernels, on_device(): pl.pallas_call(functools.partial(kernel, nx, ny, levels, rows, cols), out...  34.1 us
    unnamed x1, local copies, waits for them, and re-layouts  1.32 us

profile of v8, /device:TPU:0, one launch (start us, length us, event | category | flops | bytes accessed | tf_op | source)
XLA Modules:
  0.0 35.4 jit_solution(11641193752432730820)
XLA Ops:
  0.0 34.1 %shard_map.64 = f32[8,512,128]{2,1,0:T(8,128)S(1)} custom-call(s32[8]{0:T(128)} %steps_hbm.1, f32[8]{0:T(128)} %rate_x_hbm.1, f32[8]{0:T(128)} %rate_y_hbm.1, f32[8,512,128]{2,1,0:T(8,128)} %inc_hbm.1, f32[8,512,128]{2,1,0:T(8,128)} %dev_hbm.1, s32[8,512,128]{2,1,0:T(8,128)} %sea_hbm.1), custom_call_target="tpu_custom_call" | custom-call | tf_op jit(solution)/shard_map/pallas_call | solution.py:624
  34.1 1.3 %copy.8 = f32[8,512,128]{2,1,0:T(8,128)} copy(f32[8,512,128]{2,1,0:T(8,128)S(1)} %shard_map.64) | data formatting | bytes 4194304
